TPU v7x, 32 devices: a whole 2x2x4 slice. The times are simulated.
32 devices in a mesh: facet: 8 (over z, x), freq: 4 (over y, core).
Axes of the slice: x: 2, y: 2, z: 4, core: 2. Of those that a mesh axis runs over, the one named last changes fastest.
Arguments:
- facet_image: bfloat16 [8, 2, 128, 4096], P('facet', None, 'freq'), may hold values from -6 to 6
- facet_offsets: int32 [8, 2], replicated, may hold values from 0 to 32767
- subgrid_rows: int32 [8], replicated, may hold values from 0 to 32767
- column_offset: int32 [1], replicated, may hold values from 0 to 32767
- uv_coords: int32 [2, 64, 8, 512], P(None, ('freq', 'facet')), may hold values from 0 to 255
- observed: bfloat16 [2, 64, 8, 512], P(None, ('freq', 'facet')), may hold values from -6 to 6
Outputs:
- image_residual: bfloat16 [8, 2, 128, 4096], P('facet', None, 'freq')
- residual_vis: bfloat16 [2, 64, 8, 512], P(None, ('freq', 'facet'))
All inputs are finite; a program needn't handle non-finite values.
Results may differ from a plain program's by a relative error of at most 0.024.
Values may be sent and summed in bfloat16 or wider, within the bound.
No kernel may reach another device: no remote copies, remote signals or barrier semaphores. Data moves between devices by JAX's collectives and lax.ppermute only.
A program may use at most 64 MiB of HBM per device.

v0:
```python
import functools
import math

import jax
import jax.numpy as jnp
from jax import lax
from jax.experimental import pallas as pl
from jax.experimental.pallas import tpu as pltpu
from jax.sharding import PartitionSpec as P

IMAGE = 32768
CONTRIB = 128
SUBGRID = 256
PATCH = 32
SIDE = 8
STEP = 128
PERIOD = 256
LANES = 128
MASK = IMAGE - 1

F32 = jnp.float32
BF16 = jnp.bfloat16


def iota(shape, axis):
    return lax.broadcasted_iota(jnp.int32, shape, axis)


def cis(turns):
    turns = turns & MASK
    quarter = (turns + IMAGE // 8) >> 13
    x = (turns - (quarter << 13)).astype(F32) * (2.0 * math.pi / IMAGE)
    x2 = x * x
    sine = x * (1.0 + x2 * (-1.0 / 6 + x2 * (1.0 / 120 - x2 * (1.0 / 5040))))
    cosine = 1.0 + x2 * (-0.5 + x2 * (1.0 / 24 + x2 * (-1.0 / 720 + x2 * (1.0 / 40320))))
    odd = (quarter & 1) == 1
    real = jnp.where(odd, sine, cosine)
    imag = jnp.where(odd, cosine, sine)
    real = jnp.where(((quarter + 1) & 2) == 2, -real, real)
    imag = jnp.where((quarter & 2) == 2, -imag, imag)
    return real, imag


def times(ar, ai, br, bi):
    return ar * br - ai * bi, ar * bi + ai * br


def block(rows):
    return jnp.concatenate([jnp.concatenate(row, axis=1) for row in rows], axis=0)


def dot(left, right):
    return lax.dot_general(left, right, (((1,), (0,)), ((), ())), preferred_element_type=F32)


def dot_t(left, right):
    return lax.dot_general(left, right, (((1,), (1,)), ((), ())), preferred_element_type=F32)


def column_tables(column, first, extent):
    col_step = IMAGE // extent
    far_count = extent // LANES
    near = ((column + col_step * iota((LANES, CONTRIB), 1)) & MASK) * iota((LANES, CONTRIB), 0)
    shape = (far_count, CONTRIB)
    far = ((column + col_step * iota(shape, 1)) & MASK) * ((first + LANES * iota(shape, 0)) & MASK)
    return cis(-near), cis(-far)


def near_weights(near):
    real, imag = near
    return block([[real, imag], [-imag, real]]).astype(BF16)


def column_kernel(column_ref, offsets_ref, image_ref, out_ref, left_ref):
    rows, extent = image_ref.shape[2:]
    far_count = extent // LANES
    first = offsets_ref[lax.axis_index("facet"), 1]
    near, (far_real, far_imag) = column_tables(column_ref[0], first, extent)
    for y1 in range(far_count):
        here = pl.ds(y1 * rows, rows)
        there = pl.ds(y1 * LANES, LANES)
        left_ref[here, :LANES] = image_ref[0, 0, :, there]
        left_ref[here, LANES:] = image_ref[0, 1, :, there]
    value = dot(left_ref[...], near_weights(near))
    real = jnp.zeros((rows, CONTRIB), F32)
    imag = jnp.zeros((rows, CONTRIB), F32)
    for y1 in range(far_count):
        part = value[y1 * rows : (y1 + 1) * rows]
        pr, pi = times(
            part[:, :CONTRIB], part[:, CONTRIB:], far_real[y1 : y1 + 1], far_imag[y1 : y1 + 1]
        )
        real += pr
        imag += pi
    scale = 1.0 / math.sqrt(extent)
    out_ref[0] = (real * scale).astype(BF16)
    out_ref[1] = (imag * scale).astype(BF16)


def spread_kernel(starts_ref, offsets_ref, piece_ref, out_ref):
    parts, _, rows, _ = piece_ref.shape
    facet_rows = parts * rows
    row_step = IMAGE // facet_rows
    block_rows = out_ref.shape[2]
    owners = SUBGRID // block_rows
    per_freq = out_ref.shape[0] // owners
    first = offsets_ref[lax.axis_index("facet"), 0]
    right = jnp.concatenate([piece_ref[q, ri] for ri in range(2) for q in range(parts)], axis=0)
    shape = (CONTRIB, facet_rows)
    contribs = []
    for j in range(per_freq):
        start = starts_ref[lax.axis_index("freq") * per_freq + j]
        turns = ((start + row_step * iota(shape, 0)) & MASK) * ((first + iota(shape, 1)) & MASK)
        rr, ri = cis(-turns)
        both = dot(block([[rr, -ri], [ri, rr]]).astype(BF16), right)
        contribs.append((both * (1.0 / math.sqrt(facet_rows))).astype(BF16))
    shape = (SUBGRID, CONTRIB)
    sr, si = cis(iota(shape, 0) * ((STEP * iota(shape, 1) + first) & MASK))
    spread = dot(
        block([[sr, -si], [si, sr]]).astype(BF16), jnp.concatenate(contribs, axis=1)
    ).astype(BF16)
    for j in range(per_freq):
        for o in range(owners):
            for ri in range(2):
                top = ri * SUBGRID + o * block_rows
                out_ref[j * owners + o, ri] = spread[
                    top : top + block_rows, j * CONTRIB : (j + 1) * CONTRIB
                ]


def patch_rows_of(row, stride):
    turn = IMAGE // PERIOD
    base = cis(iota((8, row.shape[1]), 0) * row * turn)
    blocks = [base]
    for _ in range(PATCH // 8 - 1):
        blocks.append(times(*blocks[-1], *stride))
    return (
        jnp.concatenate([b[0] for b in blocks], axis=0),
        jnp.concatenate([b[1] for b in blocks], axis=0),
    )


def grid_kernel(
    offsets_ref, in_ref, coords_ref, seen_ref, out_ref, res_ref, left_ref, back_ref, narrow_ref
):
    facets, _, block_rows, _ = in_ref.shape
    patch_rows = coords_ref.shape[1]
    vis = coords_ref.shape[3]
    turn = IMAGE // PERIOD
    shape = (facets, SUBGRID)
    firsts = jnp.zeros(shape, jnp.int32)
    for f in range(facets):
        firsts = jnp.where(iota(shape, 0) == f, offsets_ref[f, 1], firsts)
    shift_real, shift_imag = cis(firsts * iota(shape, 1))
    shape = (CONTRIB, SUBGRID)
    tr, ti = cis(iota(shape, 0) * iota(shape, 1) * STEP)
    weights = block([[tr, ti], [-ti, tr]]).astype(BF16)
    for f in range(facets):
        here = pl.ds(f * block_rows, block_rows)
        left_ref[here, :CONTRIB] = in_ref[f, 0]
        left_ref[here, CONTRIB:] = in_ref[f, 1]
    wide = dot(left_ref[...], weights)
    grid_real = jnp.zeros((block_rows, SUBGRID), F32)
    grid_imag = jnp.zeros((block_rows, SUBGRID), F32)
    for f in range(facets):
        part = wide[f * block_rows : (f + 1) * block_rows]
        pr, pi = times(
            part[:, :SUBGRID], part[:, SUBGRID:], shift_real[f : f + 1], shift_imag[f : f + 1]
        )
        grid_real += pr
        grid_imag += pi
    grid_real = (grid_real * (1.0 / CONTRIB)).astype(BF16).astype(F32)
    grid_imag = (grid_imag * (1.0 / CONTRIB)).astype(BF16).astype(F32)
    group = LANES // PATCH
    own = (iota((LANES, LANES), 0) // PATCH) == (iota((LANES, LANES), 1) // PATCH)
    factor = 1.0 / math.sqrt(vis)
    for p in range(patch_rows):
        strides = [cis(coords_ref[axis, p] * (8 * turn)) for axis in range(2)]
        for h in range(SIDE // group):
            tables = []
            for axis in range(2):
                made = [
                    patch_rows_of(
                        coords_ref[axis, p, pl.ds(c, 1), :],
                        (strides[axis][0][c : c + 1], strides[axis][1][c : c + 1]),
                    )
                    for c in range(h * group, (h + 1) * group)
                ]
                tables.append(
                    tuple(jnp.concatenate([m[ri] for m in made], axis=0) for ri in range(2))
                )
            (ur, ui), (vr, vi) = tables
            cells = (slice(p * PATCH, (p + 1) * PATCH), slice(h * LANES, (h + 1) * LANES))
            mr, mi = (
                jnp.where(own, jnp.concatenate([grid[cells]] * group, axis=0), 0.0)
                for grid in (grid_real, grid_imag)
            )
            ev = jnp.concatenate([vr, vi], axis=0).astype(BF16)
            inner = dot(block([[mr, -mi], [mi, mr]]).astype(BF16), ev)
            ir, ii = times(ur, ui, inner[:LANES], inner[LANES:])
            wr, wi = [], []
            for c in range(group):
                rows = slice(c * PATCH, (c + 1) * PATCH)
                at = h * group + c
                res = []
                for ri, value in enumerate((ir, ii)):
                    model = jnp.sum(value[rows], axis=0, keepdims=True) * (1.0 / PATCH)
                    seen = seen_ref[ri, p, pl.ds(at, 1), :].astype(F32)
                    rounded = (seen - model).astype(BF16)
                    res_ref[ri, p, pl.ds(at, 1), :] = rounded
                    res.append(rounded.astype(F32))
                wr.append(res[0] * ur[rows] + res[1] * ui[rows])
                wi.append(res[1] * ur[rows] - res[0] * ui[rows])
            back = dot_t(jnp.concatenate(wr + wi, axis=0).astype(BF16), ev)
            br = back[:LANES, :LANES] + back[LANES:, LANES:]
            bi = back[LANES:, :LANES] - back[:LANES, LANES:]
            for ri, value in enumerate((br, bi)):
                value = jnp.where(own, value, 0.0)
                total = sum(value[c * PATCH : (c + 1) * PATCH] for c in range(group))
                back_ref[ri, cells[0], cells[1]] = (total * factor).astype(BF16).astype(F32)
    for f in range(facets):
        here = pl.ds(f * block_rows, block_rows)
        nr, ni = times(
            back_ref[0], back_ref[1], shift_real[f : f + 1], -shift_imag[f : f + 1]
        )
        narrow_ref[here, :SUBGRID] = nr.astype(BF16)
        narrow_ref[here, SUBGRID:] = ni.astype(BF16)
    narrowed = dot_t(narrow_ref[...], weights).astype(BF16)
    for f in range(facets):
        for ri in range(2):
            out_ref[f, ri] = narrowed[
                f * block_rows : (f + 1) * block_rows, ri * CONTRIB : (ri + 1) * CONTRIB
            ]


def gather_kernel(starts_ref, offsets_ref, in_ref, out_ref):
    parts, _, rows, _ = out_ref.shape
    facet_rows = parts * rows
    row_step = IMAGE // facet_rows
    block_rows = in_ref.shape[2]
    owners = SUBGRID // block_rows
    per_freq = in_ref.shape[0] // owners
    first = offsets_ref[lax.axis_index("facet"), 0]
    shape = (CONTRIB, SUBGRID)
    sr, si = cis(iota(shape, 1) * ((STEP * iota(shape, 0) + first) & MASK))
    right = block(
        [
            [
                jnp.concatenate([in_ref[j * owners + o, ri] for o in range(owners)], axis=0)
                for j in range(per_freq)
            ]
            for ri in range(2)
        ]
    )
    adjoint = dot(block([[sr, si], [-si, sr]]).astype(BF16), right)
    adjoint = (adjoint * (1.0 / SUBGRID)).astype(BF16)
    shape = (facet_rows, CONTRIB)
    total = jnp.zeros((2 * facet_rows, CONTRIB), F32)
    for j in range(per_freq):
        start = starts_ref[lax.axis_index("freq") * per_freq + j]
        turns = ((start + row_step * iota(shape, 1)) & MASK) * ((first + iota(shape, 0)) & MASK)
        rr, ri = cis(-turns)
        total += dot(
            block([[rr, ri], [-ri, rr]]).astype(BF16), adjoint[:, j * CONTRIB : (j + 1) * CONTRIB]
        )
    total = total.astype(BF16)
    for q in range(parts):
        for ri in range(2):
            top = ri * facet_rows + q * rows
            out_ref[q, ri] = total[top : top + rows]


def image_kernel(subgrids, column_ref, offsets_ref, in_ref, out_ref, left_ref):
    parts = in_ref.shape[0]
    rows, extent = out_ref.shape[2:]
    far_count = extent // LANES
    first = offsets_ref[lax.axis_index("facet"), 1]
    near, (far_real, far_imag) = column_tables(column_ref[0], first, extent)
    scale = 1.0 / math.sqrt(subgrids * CONTRIB)
    real, imag = (
        sum(in_ref[q, ri].astype(F32) for q in range(parts)) * scale for ri in range(2)
    )
    for y1 in range(far_count):
        here = pl.ds(y1 * rows, rows)
        ar, ai = times(real, imag, far_real[y1 : y1 + 1], -far_imag[y1 : y1 + 1])
        left_ref[here, :CONTRIB] = ar.astype(BF16)
        left_ref[here, CONTRIB:] = ai.astype(BF16)
    value = dot_t(left_ref[...], near_weights(near)) * (1.0 / math.sqrt(CONTRIB))
    value = value.astype(BF16)
    for y1 in range(far_count):
        for ri in range(2):
            out_ref[0, ri, :, pl.ds(y1 * LANES, LANES)] = value[
                y1 * rows : (y1 + 1) * rows, ri * LANES : (ri + 1) * LANES
            ]


def call(kernel, name, small, operands, outs, scratch=()):
    smem = pl.BlockSpec(memory_space=pltpu.SMEM)
    vmem = pl.BlockSpec(memory_space=pltpu.VMEM)
    return pl.pallas_call(
        kernel,
        name=name,
        out_shape=outs,
        in_specs=[smem] * len(small) + [vmem] * len(operands),
        out_specs=jax.tree.map(lambda _: vmem, outs),
        scratch_shapes=list(scratch),
        compiler_params=pltpu.CompilerParams(vmem_limit_bytes=40 * 1024 * 1024),
    )(*small, *operands)


def on_device(facet_image, facet_offsets, subgrid_rows, column_offset, uv_coords, observed):
    shape = jax.ShapeDtypeStruct
    rows, extent = facet_image.shape[2:]
    facets = lax.axis_size("facet")
    parts = lax.axis_size("freq")
    subgrids = subgrid_rows.shape[0]
    patch_rows = uv_coords.shape[1]
    block_rows = patch_rows * PATCH
    far_rows = extent // LANES * rows
    transformed = call(
        column_kernel,
        "column",
        (column_offset, facet_offsets),
        (facet_image,),
        shape((2, rows, CONTRIB), BF16),
        (pltpu.VMEM((far_rows, 2 * LANES), BF16),),
    )
    piece = lax.all_gather(transformed, "freq", axis=0, tiled=False)
    outgoing = call(
        spread_kernel,
        "spread",
        (subgrid_rows, facet_offsets),
        (piece,),
        shape((facets, 2, block_rows, CONTRIB), BF16),
    )
    incoming = lax.all_to_all(outgoing, "facet", split_axis=0, concat_axis=0, tiled=True)
    narrowed, residual_vis = call(
        grid_kernel,
        "grid",
        (facet_offsets,),
        (incoming, uv_coords, observed),
        (shape(incoming.shape, BF16), shape(observed.shape, BF16)),
        (
            pltpu.VMEM((facets * block_rows, 2 * CONTRIB), BF16),
            pltpu.VMEM((2, block_rows, SUBGRID), F32),
            pltpu.VMEM((facets * block_rows, 2 * SUBGRID), BF16),
        ),
    )
    returned = lax.all_to_all(narrowed, "facet", split_axis=0, concat_axis=0, tiled=True)
    partial = call(
        gather_kernel,
        "gather",
        (subgrid_rows, facet_offsets),
        (returned,),
        shape((parts, 2, rows, CONTRIB), BF16),
    )
    shared = lax.all_to_all(partial, "freq", split_axis=0, concat_axis=0, tiled=True)
    image_residual = call(
        functools.partial(image_kernel, subgrids),
        "image",
        (column_offset, facet_offsets),
        (shared,),
        shape(facet_image.shape, BF16),
        (pltpu.VMEM((far_rows, 2 * LANES), BF16),),
    )
    return (image_residual, residual_vis)


def solution(mesh):
    return jax.shard_map(
        on_device,
        mesh=mesh,
        in_specs=(
            P("facet", None, "freq", None),
            P(),
            P(),
            P(),
            P(None, ("freq", "facet"), None, None),
            P(None, ("freq", "facet"), None, None),
        ),
        out_specs=(P("facet", None, "freq", None), P(None, ("freq", "facet"), None, None)),
        check_vma=False,
    )
```

profile of v0, /device:TPU:0, one launch (start us, length us, event | category | flops | bytes accessed | tf_op | source)
XLA Modules:
  0.0 53.2 jit_solution(13643276781479687707)
XLA Ops:
  0.6 0.0 copy-start.4
  1.3 0.0 copy-done.4
  1.3 0.1 copy.17.offsets_ref
  1.4 0.0 copy-start
  1.4 1.0 %copy-done = bf16[1,2,32,4096]{3,2,1,0:T(8,128)(2,1)S(1)} copy-done((bf16[1,2,32,4096]{3,2,1,0:T(8,128)(2,1)S(1)}, bf16[1,2,32,4096]{3,2,1,0:T(8,128)(2,1)}, u32[]{:S(2)}) %copy-start) | copy-done | bytes 524312
  2.4 1.0 %column.1 = bf16[2,32,128]{2,1,0:T(8,128)(2,1)S(1)} custom-call(s32[1]{0:T(128)S(6)} %copy.18.column_ref, s32[8,2]{1,0:T(8,128)S(1)} %copy.17.offsets_ref, bf16[1,2,32,4096]{3,2,1,0:T(8,128)(2,1)S(1)} %copy-done), custom_call_target="tpu_custom_call" | custom-call | tf_op jit(solution)/shard_map/column/pallas_call | solution.py:299
  3.5 6.2 %all-gather = bf16[8,32,128]{2,1,0:T(8,128)(2,1)S(1)} all-gather(bf16[2,32,128]{2,1,0:T(8,128)(2,1)S(1)} %column.1), channel_id=2, replica_groups=mesh['facet'=8,'freq'=4] {'freq'}, dimensions={0}, use_global_device_ids=true | all-gather | bytes 81920 | tf_op jit(solution)/shard_map/all_gather | solution.py:327
  9.7 0.0 copy-start.3
  9.7 0.7 %copy-done.3 = s32[8]{0:T(128)S(1)} copy-done((s32[8]{0:T(128)S(1)}, s32[8]{0:T(128)}, u32[]{:S(2)}) %copy-start.3) | copy-done | bytes 56
  10.3 1.2 %spread.1 = bf16[8,2,64,128]{3,2,1,0:T(8,128)(2,1)S(1)} custom-call(s32[8]{0:T(128)S(1)} %copy-done.3, s32[8,2]{1,0:T(8,128)S(1)} %copy.17.offsets_ref, bf16[4,2,32,128]{3,2,1,0:T(8,128)(2,1)S(1)} %bitcast.1), custom_call_target="tpu_custom_call" | custom-call | tf_op jit(solution)/shard_map/spread/pallas_call | solution.py:299
  11.5 0.0 copy-start.1
  11.6 0.0 copy-start.2
  11.6 15.7 %all_to_all.15.in_ref = bf16[8,2,64,128]{3,2,1,0:T(8,128)(2,1)S(1)} all-to-all(bf16[8,2,64,128]{3,2,1,0:T(8,128)(2,1)S(1)} %spread.1), channel_id=1, replica_groups=mesh['facet'=8,'freq'=4] {'facet'}, dimensions={0} | all-to-all | bytes 524288 | tf_op jit(solution)/shard_map/all_to_all | solution.py:335
  27.2 0.0 copy-done.1
  27.2 0.0 copy-done.2
  27.2 3.7 %grid.1 = (bf16[8,2,64,128]{3,2,1,0:T(8,128)(2,1)S(1)}, bf16[2,2,8,512]{3,2,1,0:T(8,128)(2,1)}) custom-call(s32[8,2]{1,0:T(8,128)S(1)} %copy.17.offsets_ref, bf16[8,2,64,128]{3,2,1,0:T(8,128)(2,1)S(1)} %all_to_all.15.in_ref, s32[2,2,8,512]{3,2,1,0:T(8,128)S(1)} %copy-done.1, bf16[2,2,8,512]{3,2,1,0:T(8,128)(2,1)S(1)} %copy-done.2), custom_call_target="tpu_custom_call" | custom-call | tf_op jit(solution)/shard_map/grid/pallas_call | solution.py:299
  31.0 12.4 %all_to_all.16.in_ref = bf16[8,2,64,128]{3,2,1,0:T(8,128)(2,1)S(1)} all-to-all(bf16[8,2,64,128]{3,2,1,0:T(8,128)(2,1)S(1)} %get-tuple-element.4), channel_id=1, replica_groups=mesh['facet'=8,'freq'=4] {'facet'}, dimensions={0} | all-to-all | bytes 524288 | tf_op jit(solution)/shard_map/all_to_all | solution.py:348
  43.3 1.3 %gather.1 = bf16[4,2,32,128]{3,2,1,0:T(8,128)(2,1)S(1)} custom-call(s32[8]{0:T(128)S(1)} %copy-done.3, s32[8,2]{1,0:T(8,128)S(1)} %copy.17.offsets_ref, bf16[8,2,64,128]{3,2,1,0:T(8,128)(2,1)S(1)} %all_to_all.16.in_ref), custom_call_target="tpu_custom_call" | custom-call | tf_op jit(solution)/shard_map/gather/pallas_call | solution.py:299
  44.6 6.7 %all_to_all.17.in_ref = bf16[4,2,32,128]{3,2,1,0:T(8,128)(2,1)S(1)} all-to-all(bf16[4,2,32,128]{3,2,1,0:T(8,128)(2,1)S(1)} %gather.1), channel_id=1, replica_groups=mesh['facet'=8,'freq'=4] {'freq'}, dimensions={0} | all-to-all | bytes 131072 | tf_op jit(solution)/shard_map/all_to_all | solution.py:356
  51.3 1.9 %image.1 = bf16[1,2,32,4096]{3,2,1,0:T(8,128)(2,1)} custom-call(s32[1]{0:T(128)S(6)} %copy.18.column_ref, s32[8,2]{1,0:T(8,128)S(1)} %copy.17.offsets_ref, bf16[4,2,32,128]{3,2,1,0:T(8,128)(2,1)S(1)} %all_to_all.17.in_ref), custom_call_target="tpu_custom_call" | custom-call | tf_op jit(solution)/shard_map/image/pallas_call | solution.py:299
Async XLA Ops:
  0.6 0.7 %copy-start.4 = (s32[8,2]{0,1:T(2,128)S(1)}, s32[8,2]{0,1:T(2,128)}, u32[]{:S(2)}) copy-start(s32[8,2]{0,1:T(2,128)} %param.7) | copy-start | bytes 196
  1.4 1.0 %copy-start = (bf16[1,2,32,4096]{3,2,1,0:T(8,128)(2,1)S(1)}, bf16[1,2,32,4096]{3,2,1,0:T(8,128)(2,1)}, u32[]{:S(2)}) copy-start(bf16[1,2,32,4096]{3,2,1,0:T(8,128)(2,1)} %image_ref.1) | copy-start | bytes 1572868
  9.7 0.7 %copy-start.3 = (s32[8]{0:T(128)S(1)}, s32[8]{0:T(128)}, u32[]{:S(2)}) copy-start(s32[8]{0:T(128)} %starts_ref.3) | copy-start | bytes 100
  11.5 15.7 %copy-start.1 = (s32[2,2,8,512]{3,2,1,0:T(8,128)S(1)}, s32[2,2,8,512]{3,2,1,0:T(8,128)}, u32[]{:S(2)}) copy-start(s32[2,2,8,512]{3,2,1,0:T(8,128)} %coords_ref.1) | copy-start | bytes 196612
  11.6 15.7 %copy-start.2 = (bf16[2,2,8,512]{3,2,1,0:T(8,128)(2,1)S(1)}, bf16[2,2,8,512]{3,2,1,0:T(8,128)(2,1)}, u32[]{:S(2)}) copy-start(bf16[2,2,8,512]{3,2,1,0:T(8,128)(2,1)} %seen_ref.1) | copy-start | bytes 98308
where the time goes:
time: 53.6 us; the launch traced here: 53.2 us
  blocking collectives  41 us (76%)
  Pallas kernels  9.12 us (17%)
  local copies, waits for them, and re-layouts  1.8 us (3%)
  between operations  1.35 us (3%)
    all_to_all x1, blocking collectives, on_device(): lax.all_to_all(outgoing, 'facet', split_axis=0, concat_axis=0, tiled=True)  15.7 us
    all_to_all x1, blocking collectives, on_device(): lax.all_to_all(narrowed, 'facet', split_axis=0, concat_axis=0, tiled=True)  12.4 us
    pallas_call x5, Pallas kernels, call(): pl.pallas_call(kernel, name=name, out_shape=outs, in_specs=[smem] * len(s...  9.12 us
    all_to_all x1, blocking collectives, on_device(): lax.all_to_all(partial, 'freq', split_axis=0, concat_axis=0, tiled=True)  6.71 us
    all_gather x1, blocking collectives, on_device(): piece = lax.all_gather(transformed, 'freq', axis=0, tiled=False)  6.21 us
    unnamed x11, local copies, waits for them, and re-layouts  1.8 us

commit v1 on v0

--- a/solution.py
+++ b/solution.py
@@ -57,6 +57,10 @@
     return lax.dot_general(left, right, (((1,), (1,)), ((), ())), preferred_element_type=F32)
 
 
+def dot_0(left, right):
+    return lax.dot_general(left, right, (((0,), (0,)), ((), ())), preferred_element_type=F32)
+
+
 def column_tables(column, first, extent):
     col_step = IMAGE // extent
     far_count = extent // LANES
@@ -74,7 +78,7 @@
 def column_kernel(column_ref, offsets_ref, image_ref, out_ref, left_ref):
     rows, extent = image_ref.shape[2:]
     far_count = extent // LANES
-    first = offsets_ref[lax.axis_index("facet"), 1]
+    first = offsets_ref[1, lax.axis_index("facet")]
     near, (far_real, far_imag) = column_tables(column_ref[0], first, extent)
     for y1 in range(far_count):
         here = pl.ds(y1 * rows, rows)
@@ -92,39 +96,35 @@
         real += pr
         imag += pi
     scale = 1.0 / math.sqrt(extent)
-    out_ref[0] = (real * scale).astype(BF16)
-    out_ref[1] = (imag * scale).astype(BF16)
-
-
-def spread_kernel(starts_ref, offsets_ref, piece_ref, out_ref):
-    parts, _, rows, _ = piece_ref.shape
-    facet_rows = parts * rows
-    row_step = IMAGE // facet_rows
-    block_rows = out_ref.shape[2]
+    both = jnp.stack([(real * scale).astype(BF16), (imag * scale).astype(BF16)])
+    for copy in range(out_ref.shape[0]):
+        out_ref[copy] = both
+
+
+def row_tables(starts_ref, offsets_ref, facets, block_rows, facet_rows):
+    half_step = IMAGE // facet_rows // 2
     owners = SUBGRID // block_rows
-    per_freq = out_ref.shape[0] // owners
-    first = offsets_ref[lax.axis_index("facet"), 0]
-    right = jnp.concatenate([piece_ref[q, ri] for ri in range(2) for q in range(parts)], axis=0)
-    shape = (CONTRIB, facet_rows)
-    contribs = []
-    for j in range(per_freq):
-        start = starts_ref[lax.axis_index("freq") * per_freq + j]
-        turns = ((start + row_step * iota(shape, 0)) & MASK) * ((first + iota(shape, 1)) & MASK)
-        rr, ri = cis(-turns)
-        both = dot(block([[rr, -ri], [ri, rr]]).astype(BF16), right)
-        contribs.append((both * (1.0 / math.sqrt(facet_rows))).astype(BF16))
-    shape = (SUBGRID, CONTRIB)
-    sr, si = cis(iota(shape, 0) * ((STEP * iota(shape, 1) + first) & MASK))
-    spread = dot(
-        block([[sr, -si], [si, sr]]).astype(BF16), jnp.concatenate(contribs, axis=1)
-    ).astype(BF16)
-    for j in range(per_freq):
-        for o in range(owners):
-            for ri in range(2):
-                top = ri * SUBGRID + o * block_rows
-                out_ref[j * owners + o, ri] = spread[
-                    top : top + block_rows, j * CONTRIB : (j + 1) * CONTRIB
-                ]
+    index = lax.axis_index("freq") * lax.axis_size("facet") + lax.axis_index("facet")
+    start = starts_ref[index // owners]
+    shape = (block_rows, facet_rows)
+    row = (index % owners) * block_rows + iota(shape, 0)
+    half = (STEP // 2) * row - half_step * iota(shape, 1)
+    top = cis(CONTRIB * half)[1]
+    low = cis(half)[1]
+    even = (half & (IMAGE // 2 - 1)) == 0
+    limit = jnp.where((half & MASK) == 0, float(CONTRIB), -float(CONTRIB))
+    kernel = jnp.where(even, limit, top / jnp.where(even, 1.0, low))
+    tables = []
+    for f in range(facets):
+        first = offsets_ref[0, f]
+        shift = (facet_rows - first % facet_rows) % facet_rows
+        rolled = pltpu.roll(kernel, shift, 1)
+        place = first + iota(shape, 1)
+        half = (STEP // 2) * row - half_step * (place & (facet_rows - 1))
+        turns = row * first - start * (place & MASK) + (CONTRIB - 1) * half
+        real, imag = cis(turns)
+        tables.append((rolled * real, rolled * imag))
+    return tables
 
 
 def patch_rows_of(row, stride):
@@ -140,24 +140,52 @@
 
 
 def grid_kernel(
-    offsets_ref, in_ref, coords_ref, seen_ref, out_ref, res_ref, left_ref, back_ref, narrow_ref
+    starts_ref,
+    offsets_ref,
+    own_ref,
+    other_ref,
+    coords_ref,
+    seen_ref,
+    keep_ref,
+    give_ref,
+    res_ref,
+    pieces_ref,
+    rows_ref,
+    left_ref,
+    back_ref,
+    narrow_ref,
 ):
-    facets, _, block_rows, _ = in_ref.shape
+    facets = offsets_ref.shape[1]
+    pairs = own_ref.shape[0] // facets
+    piece_rows = own_ref.shape[2]
+    facet_rows = 2 * pairs * piece_rows
     patch_rows = coords_ref.shape[1]
+    block_rows = patch_rows * PATCH
     vis = coords_ref.shape[3]
     turn = IMAGE // PERIOD
+    core = lax.axis_index("freq") % 2
+    for f in range(facets):
+        for y in range(pairs):
+            for ri in range(2):
+                pieces_ref[f, ri, 2 * y + core] = own_ref[y * facets + f, ri]
+                pieces_ref[f, ri, 2 * y + 1 - core] = other_ref[y * facets + f, ri]
+    tables = row_tables(starts_ref, offsets_ref, facets, block_rows, facet_rows)
+    scale = 1.0 / math.sqrt(facet_rows)
+    for f, (mr, mi) in enumerate(tables):
+        mr, mi = mr.astype(BF16), mi.astype(BF16)
+        rows_ref[f] = block([[mr, -mi], [mi, mr]])
+        part = dot(rows_ref[f], pieces_ref[f].reshape(2 * facet_rows, CONTRIB)) * scale
+        here = pl.ds(f * block_rows, block_rows)
+        left_ref[here, :CONTRIB] = part[:block_rows].astype(BF16)
+        left_ref[here, CONTRIB:] = part[block_rows:].astype(BF16)
     shape = (facets, SUBGRID)
     firsts = jnp.zeros(shape, jnp.int32)
     for f in range(facets):
-        firsts = jnp.where(iota(shape, 0) == f, offsets_ref[f, 1], firsts)
+        firsts = jnp.where(iota(shape, 0) == f, offsets_ref[1, f], firsts)
     shift_real, shift_imag = cis(firsts * iota(shape, 1))
     shape = (CONTRIB, SUBGRID)
     tr, ti = cis(iota(shape, 0) * iota(shape, 1) * STEP)
     weights = block([[tr, ti], [-ti, tr]]).astype(BF16)
-    for f in range(facets):
-        here = pl.ds(f * block_rows, block_rows)
-        left_ref[here, :CONTRIB] = in_ref[f, 0]
-        left_ref[here, CONTRIB:] = in_ref[f, 1]
     wide = dot(left_ref[...], weights)
     grid_real = jnp.zeros((block_rows, SUBGRID), F32)
     grid_imag = jnp.zeros((block_rows, SUBGRID), F32)
@@ -226,54 +254,21 @@
         narrow_ref[here, SUBGRID:] = ni.astype(BF16)
     narrowed = dot_t(narrow_ref[...], weights).astype(BF16)
     for f in range(facets):
-        for ri in range(2):
-            out_ref[f, ri] = narrowed[
-                f * block_rows : (f + 1) * block_rows, ri * CONTRIB : (ri + 1) * CONTRIB
-            ]
-
-
-def gather_kernel(starts_ref, offsets_ref, in_ref, out_ref):
-    parts, _, rows, _ = out_ref.shape
-    facet_rows = parts * rows
-    row_step = IMAGE // facet_rows
-    block_rows = in_ref.shape[2]
-    owners = SUBGRID // block_rows
-    per_freq = in_ref.shape[0] // owners
-    first = offsets_ref[lax.axis_index("facet"), 0]
-    shape = (CONTRIB, SUBGRID)
-    sr, si = cis(iota(shape, 1) * ((STEP * iota(shape, 0) + first) & MASK))
-    right = block(
-        [
-            [
-                jnp.concatenate([in_ref[j * owners + o, ri] for o in range(owners)], axis=0)
-                for j in range(per_freq)
-            ]
-            for ri in range(2)
-        ]
-    )
-    adjoint = dot(block([[sr, si], [-si, sr]]).astype(BF16), right)
-    adjoint = (adjoint * (1.0 / SUBGRID)).astype(BF16)
-    shape = (facet_rows, CONTRIB)
-    total = jnp.zeros((2 * facet_rows, CONTRIB), F32)
-    for j in range(per_freq):
-        start = starts_ref[lax.axis_index("freq") * per_freq + j]
-        turns = ((start + row_step * iota(shape, 1)) & MASK) * ((first + iota(shape, 0)) & MASK)
-        rr, ri = cis(-turns)
-        total += dot(
-            block([[rr, ri], [-ri, rr]]).astype(BF16), adjoint[:, j * CONTRIB : (j + 1) * CONTRIB]
-        )
-    total = total.astype(BF16)
-    for q in range(parts):
-        for ri in range(2):
-            top = ri * facet_rows + q * rows
-            out_ref[q, ri] = total[top : top + rows]
+        part = narrowed[f * block_rows : (f + 1) * block_rows]
+        part = jnp.concatenate([part[:, :CONTRIB], part[:, CONTRIB:]], axis=0)
+        back = (dot_0(rows_ref[f], part) * (1.0 / SUBGRID)).astype(BF16)
+        pieces_ref[f] = back.reshape(2, 2 * pairs, piece_rows, CONTRIB)
+        for y in range(pairs):
+            for ri in range(2):
+                keep_ref[y * facets + f, ri] = pieces_ref[f, ri, 2 * y + core]
+                give_ref[y * facets + f, ri] = pieces_ref[f, ri, 2 * y + 1 - core]
 
 
 def image_kernel(subgrids, column_ref, offsets_ref, in_ref, out_ref, left_ref):
     parts = in_ref.shape[0]
     rows, extent = out_ref.shape[2:]
     far_count = extent // LANES
-    first = offsets_ref[lax.axis_index("facet"), 1]
+    first = offsets_ref[1, lax.axis_index("facet")]
     near, (far_real, far_imag) = column_tables(column_ref[0], first, extent)
     scale = 1.0 / math.sqrt(subgrids * CONTRIB)
     real, imag = (
@@ -313,52 +308,54 @@
     facets = lax.axis_size("facet")
     parts = lax.axis_size("freq")
     subgrids = subgrid_rows.shape[0]
-    patch_rows = uv_coords.shape[1]
-    block_rows = patch_rows * PATCH
+    block_rows = uv_coords.shape[1] * PATCH
     far_rows = extent // LANES * rows
+    members = facets * parts // 2
+    groups = [
+        [(2 * y + c) * facets + f for y in range(parts // 2) for f in range(facets)]
+        for c in range(2)
+    ]
+    offsets = facet_offsets.T
+
+    def exchange(value):
+        return lax.all_to_all(
+            value, ("freq", "facet"), split_axis=0, concat_axis=0, axis_index_groups=groups, tiled=True
+        )
+
+    def swap(value):
+        return lax.ppermute(value, "freq", [(q, q ^ 1) for q in range(parts)])
+
+    pieces = shape((members, 2, rows, CONTRIB), BF16)
     transformed = call(
         column_kernel,
         "column",
-        (column_offset, facet_offsets),
+        (column_offset, offsets),
         (facet_image,),
-        shape((2, rows, CONTRIB), BF16),
+        pieces,
         (pltpu.VMEM((far_rows, 2 * LANES), BF16),),
     )
-    piece = lax.all_gather(transformed, "freq", axis=0, tiled=False)
-    outgoing = call(
-        spread_kernel,
-        "spread",
-        (subgrid_rows, facet_offsets),
-        (piece,),
-        shape((facets, 2, block_rows, CONTRIB), BF16),
-    )
-    incoming = lax.all_to_all(outgoing, "facet", split_axis=0, concat_axis=0, tiled=True)
-    narrowed, residual_vis = call(
+    own = exchange(transformed)
+    other = swap(own)
+    keep, give, residual_vis = call(
         grid_kernel,
         "grid",
-        (facet_offsets,),
-        (incoming, uv_coords, observed),
-        (shape(incoming.shape, BF16), shape(observed.shape, BF16)),
+        (subgrid_rows, offsets),
+        (own, other, uv_coords, observed),
+        (pieces, pieces, shape(observed.shape, BF16)),
         (
+            pltpu.VMEM((facets, 2, parts, rows, CONTRIB), BF16),
+            pltpu.VMEM((facets, 2 * block_rows, 2 * parts * rows), BF16),
             pltpu.VMEM((facets * block_rows, 2 * CONTRIB), BF16),
             pltpu.VMEM((2, block_rows, SUBGRID), F32),
             pltpu.VMEM((facets * block_rows, 2 * SUBGRID), BF16),
         ),
     )
-    returned = lax.all_to_all(narrowed, "facet", split_axis=0, concat_axis=0, tiled=True)
-    partial = call(
-        gather_kernel,
-        "gather",
-        (subgrid_rows, facet_offsets),
-        (returned,),
-        shape((parts, 2, rows, CONTRIB), BF16),
-    )
-    shared = lax.all_to_all(partial, "freq", split_axis=0, concat_axis=0, tiled=True)
+    partial = (keep.astype(F32) + swap(give).astype(F32)).astype(BF16)
     image_residual = call(
         functools.partial(image_kernel, subgrids),
         "image",
-        (column_offset, facet_offsets),
-        (shared,),
+        (column_offset, offsets),
+        (exchange(partial),),
         shape(facet_image.shape, BF16),
         (pltpu.VMEM((far_rows, 2 * LANES), BF16),),
     )

time: 53.6 us -> 45.4 us (0.85)
  blocking collectives: 41 us -> 31.5 us
  waiting for transfers between devices: 0 us -> 2.95 us
  Pallas kernels: 9.12 us -> 7.31 us
    all_gather x1 -> x0, blocking collectives: 6.21 us -> none  [on_device(): piece = lax.all_gather(transformed, 'freq', axis=0, tiled=False)]
    all_to_all x3 -> x2, blocking collectives: 34.7 us -> 31.5 us  [exchange(): lax.all_to_all(value, ('freq', 'facet'), split_axis=0, concat_axis=0, axi...]
    ppermute x0 -> x2, waiting for transfers between devices: none -> 2.95 us  [swap(): return lax.ppermute(value, 'freq', [(q, q ^ 1) for q in range(parts)])]
    pallas_call x5 -> x3, Pallas kernels: 9.12 us -> 7.31 us  [call(): pl.pallas_call(kernel, name=name, out_shape=outs, in_specs=[smem] * len(s...]
    unnamed x11 -> x10, local copies, waits for them, and re-layouts: 1.8 us -> 1.73 us
  transfers between devices with their start and end apart: 0 -> 2, of which waited for: 0 -> 2; matrix products, arithmetic and copies ran while one was open for 0% -> 0% of each run, Pallas kernels for 0% -> 0%
where the time goes in v1:
time: 45.4 us; the launch traced here: 45.1 us
  blocking collectives  31.5 us (69%)
  Pallas kernels  7.31 us (16%)
  waiting for transfers between devices  2.95 us (6%)
  local copies, waits for them, and re-layouts  1.73 us (4%)
  between operations  1.34 us (3%)
    all_to_all x2, blocking collectives, exchange(): lax.all_to_all(value, ('freq', 'facet'), split_axis=0, concat_axis=0, axi...  31.5 us
    pallas_call x3, Pallas kernels, call(): pl.pallas_call(kernel, name=name, out_shape=outs, in_specs=[smem] * len(s...  7.31 us
    ppermute x2, waiting for transfers between devices, swap(): return lax.ppermute(value, 'freq', [(q, q ^ 1) for q in range(parts)])  2.95 us
    unnamed x10, local copies, waits for them, and re-layouts  1.73 us
  transfers between devices with their start and end apart: 2, of which 2 were waited for; matrix products, arithmetic and copies ran while one was open for 0% of the time, Pallas kernels for 0%

profile of v1, /device:TPU:0, one launch (start us, length us, event | category | flops | bytes accessed | tf_op | source)
XLA Modules:
  0.0 45.1 jit_solution(10134119896786345530)
XLA Ops:
  1.3 0.0 copy-start.3
  1.3 0.7 %copy-done.3 = s32[8,2]{0,1:T(2,128)S(1)} copy-done((s32[8,2]{0,1:T(2,128)S(1)}, s32[8,2]{0,1:T(2,128)}, u32[]{:S(2)}) %copy-start.3) | copy-done | bytes 88
  2.0 0.0 copy-start
  2.0 1.0 %copy-done = bf16[1,2,32,4096]{3,2,1,0:T(8,128)(2,1)S(1)} copy-done((bf16[1,2,32,4096]{3,2,1,0:T(8,128)(2,1)S(1)}, bf16[1,2,32,4096]{3,2,1,0:T(8,128)(2,1)}, u32[]{:S(2)}) %copy-start) | copy-done | bytes 524312
  3.0 1.0 %column.1 = bf16[16,2,32,128]{3,2,1,0:T(8,128)(2,1)S(1)} custom-call(s32[1]{0:T(128)S(6)} %copy.8.column_ref, s32[2,8]{1,0:T(2,128)S(1)} %bitcast.1, bf16[1,2,32,4096]{3,2,1,0:T(8,128)(2,1)S(1)} %copy-done), custom_call_target="tpu_custom_call" | custom-call | tf_op jit(solution)/shard_map/column/pallas_call | solution.py:294
  4.0 0.0 copy-start.1
  4.0 0.0 copy-start.2
  4.0 0.0 copy-start.4
  4.0 18.1 %all_to_all.10.own_ref = bf16[16,2,32,128]{3,2,1,0:T(8,128)(2,1)S(1)} all-to-all(bf16[16,2,32,128]{3,2,1,0:T(8,128)(2,1)S(1)} %column.1), channel_id=1, replica_groups={{0,4,8,12,16,20,24,28,2,6,10,14,18,22,26,30},{1,5,9,13,17,21,25,29,3,7,..., dimensions={0} | all-to-all | bytes 524288 | tf_op jit(solution)/shard_map/all_to_all | solution.py:321
  22.2 0.0 collective-permute-start
  22.2 1.5 %collective-permute-done.other_ref = bf16[16,2,32,128]{3,2,1,0:T(8,128)(2,1)S(1)} collective-permute-done((bf16[16,2,32,128]{3,2,1,0:T(8,128)(2,1)S(1)}, bf16[16,2,32,128]{3,2,1,0:T(8,128)(2,1)S(1)}, u32[]{:S(2)}, u32[]{:S(2)}) %collective-permute-start) | collective-permute-done | bytes 262176 | tf_op jit(solution)/shard_map/ppermute | solution.py:326
  23.7 0.0 copy-done.1
  23.7 0.0 copy-done.2
  23.7 0.0 copy-done.4
  23.7 4.4 %grid.1 = (bf16[16,2,32,128]{3,2,1,0:T(8,128)(2,1)S(1)}, bf16[16,2,32,128]{3,2,1,0:T(8,128)(2,1)S(1)}, bf16[2,2,8,512]{3,2,1,0:T(8,128)(2,1)}) custom-call(s32[8]{0:T(128)S(1)} %copy-done.4, s32[2,8]{1,0:T(2,128)S(1)} %bitcast.2, bf16[16,2,32,128]{3,2,1,0:T(8,128)(2,1)S(1)} %all_to_all.10.own_ref, ...), custom_call_target="tpu_custom_call" | custom-call | tf_op jit(solution)/shard_map/grid/pallas_call | solution.py:294
  28.1 0.2 collective-permute-start.1
  28.3 1.4 %collective-permute-done.1 = bf16[16,2,32,128]{3,2,1,0:T(8,128)(2,1)S(1)} collective-permute-done((bf16[16,2,32,128]{3,2,1,0:T(8,128)(2,1)S(1)}, bf16[16,2,32,128]{3,2,1,0:T(8,128)(2,1)S(1)}, u32[]{:S(2)}, u32[]{:S(2)}) %collective-permute-start.1) | collective-permute-done | bytes 262176 | tf_op jit(solution)/shard_map/ppermute | solution.py:326
  29.7 0.1 add_convert_fusion
  29.8 13.3 %all_to_all.11.in_ref = bf16[16,2,32,128]{3,2,1,0:T(8,128)(2,1)S(1)} all-to-all(bf16[16,2,32,128]{3,2,1,0:T(8,128)(2,1)S(1)} %add_convert_fusion), channel_id=1, replica_groups={{0,4,8,12,16,20,24,28,2,6,10,14,18,22,26,30},{1,5,9,13,17,21,25,29,3,7,..., dimensions={0} | all-to-all | bytes 524288 | tf_op jit(solution)/shard_map/all_to_all | solution.py:321
  43.2 1.9 %image.1 = bf16[1,2,32,4096]{3,2,1,0:T(8,128)(2,1)} custom-call(s32[1]{0:T(128)S(6)} %copy.8.column_ref, s32[2,8]{1,0:T(2,128)S(1)} %bitcast.3, bf16[16,2,32,128]{3,2,1,0:T(8,128)(2,1)S(1)} %all_to_all.11.in_ref), custom_call_target="tpu_custom_call" | custom-call | tf_op jit(solution)/shard_map/image/pallas_call | solution.py:294
Async XLA Ops:
  1.3 0.7 %copy-start.3 = (s32[8,2]{0,1:T(2,128)S(1)}, s32[8,2]{0,1:T(2,128)}, u32[]{:S(2)}) copy-start(s32[8,2]{0,1:T(2,128)} %param.7) | copy-start | bytes 196
  2.0 1.0 %copy-start = (bf16[1,2,32,4096]{3,2,1,0:T(8,128)(2,1)S(1)}, bf16[1,2,32,4096]{3,2,1,0:T(8,128)(2,1)}, u32[]{:S(2)}) copy-start(bf16[1,2,32,4096]{3,2,1,0:T(8,128)(2,1)} %image_ref.1) | copy-start | bytes 1572868
  4.0 19.7 %copy-start.1 = (s32[2,2,8,512]{3,2,1,0:T(8,128)S(1)}, s32[2,2,8,512]{3,2,1,0:T(8,128)}, u32[]{:S(2)}) copy-start(s32[2,2,8,512]{3,2,1,0:T(8,128)} %coords_ref.1) | copy-start | bytes 196612
  4.0 19.7 %copy-start.2 = (bf16[2,2,8,512]{3,2,1,0:T(8,128)(2,1)S(1)}, bf16[2,2,8,512]{3,2,1,0:T(8,128)(2,1)}, u32[]{:S(2)}) copy-start(bf16[2,2,8,512]{3,2,1,0:T(8,128)(2,1)} %seen_ref.1) | copy-start | bytes 98308
  4.0 19.7 %copy-start.4 = (s32[8]{0:T(128)S(1)}, s32[8]{0:T(128)}, u32[]{:S(2)}) copy-start(s32[8]{0:T(128)} %starts_ref.1) | copy-start | bytes 100
  22.2 1.5 %collective-permute-start = (bf16[16,2,32,128]{3,2,1,0:T(8,128)(2,1)S(1)}, bf16[16,2,32,128]{3,2,1,0:T(8,128)(2,1)S(1)}, u32[]{:S(2)}, u32[]{:S(2)}) collective-permute-start(bf16[16,2,32,128]{3,2,1,0:T(8,128)(2,1)S(1)} %all_to_all.10.own_ref), channel_id=1, source_target_pairs={{0,1},{1,0},{2,3},{3,2},{4,5},{5,4},{6,7},{7,6},{8,9},{9,8},{10,11... | collective-permute-start | bytes 786440 | tf_op jit(solution)/shard_map/ppermute | solution.py:326
  28.1 1.6 %collective-permute-start.1 = (bf16[16,2,32,128]{3,2,1,0:T(8,128)(2,1)S(1)}, bf16[16,2,32,128]{3,2,1,0:T(8,128)(2,1)S(1)}, u32[]{:S(2)}, u32[]{:S(2)}) collective-permute-start(bf16[16,2,32,128]{3,2,1,0:T(8,128)(2,1)S(1)} %get-tuple-element.6), channel_id=1, source_target_pairs={{0,1},{1,0},{2,3},{3,2},{4,5},{5,4},{6,7},{7,6},{8,9},{9,8},{10,11... | collective-permute-start | bytes 786440 | tf_op jit(solution)/shard_map/ppermute | solution.py:326

commit v2 on v1

--- a/solution.py
+++ b/solution.py
@@ -139,53 +139,76 @@
     )
 
 
+def table_kernel(
+    starts_ref, offsets_ref, coords_ref, rows_ref, weights_ref, shift_ref, eu_ref, ev_ref
+):
+    facets = offsets_ref.shape[1]
+    patch_rows = coords_ref.shape[1]
+    block_rows = patch_rows * PATCH
+    turn = IMAGE // PERIOD
+    tables = row_tables(starts_ref, offsets_ref, facets, block_rows, rows_ref.shape[2] // 2)
+    for f, (mr, mi) in enumerate(tables):
+        mr, mi = mr.astype(BF16), mi.astype(BF16)
+        rows_ref[f] = block([[mr, -mi], [mi, mr]])
+    shape = (facets, SUBGRID)
+    firsts = jnp.zeros(shape, jnp.int32)
+    for f in range(facets):
+        firsts = jnp.where(iota(shape, 0) == f, offsets_ref[1, f], firsts)
+    shift_ref[0], shift_ref[1] = cis(firsts * iota(shape, 1))
+    shape = (CONTRIB, SUBGRID)
+    tr, ti = cis(iota(shape, 0) * iota(shape, 1) * STEP)
+    weights_ref[...] = block([[tr, ti], [-ti, tr]]).astype(BF16)
+    group = LANES // PATCH
+    for p in range(patch_rows):
+        for axis, ref in enumerate((eu_ref, ev_ref)):
+            sr, si = cis(coords_ref[axis, p] * (8 * turn))
+            for c in range(SIDE):
+                made = patch_rows_of(
+                    coords_ref[axis, p, pl.ds(c, 1), :], (sr[c : c + 1], si[c : c + 1])
+                )
+                for ri in range(2):
+                    here = pl.ds(ri * LANES + c % group * PATCH, PATCH)
+                    ref[p, c // group, here, :] = made[ri].astype(BF16)
+
+
 def grid_kernel(
-    starts_ref,
-    offsets_ref,
     own_ref,
     other_ref,
-    coords_ref,
+    rows_ref,
+    weights_ref,
+    shift_ref,
+    eu_ref,
+    ev_ref,
     seen_ref,
     keep_ref,
     give_ref,
     res_ref,
     pieces_ref,
-    rows_ref,
     left_ref,
     back_ref,
     narrow_ref,
 ):
-    facets = offsets_ref.shape[1]
+    facets = rows_ref.shape[0]
     pairs = own_ref.shape[0] // facets
     piece_rows = own_ref.shape[2]
     facet_rows = 2 * pairs * piece_rows
-    patch_rows = coords_ref.shape[1]
+    patch_rows = seen_ref.shape[1]
     block_rows = patch_rows * PATCH
-    vis = coords_ref.shape[3]
-    turn = IMAGE // PERIOD
+    vis = seen_ref.shape[3]
     core = lax.axis_index("freq") % 2
     for f in range(facets):
         for y in range(pairs):
             for ri in range(2):
                 pieces_ref[f, ri, 2 * y + core] = own_ref[y * facets + f, ri]
                 pieces_ref[f, ri, 2 * y + 1 - core] = other_ref[y * facets + f, ri]
-    tables = row_tables(starts_ref, offsets_ref, facets, block_rows, facet_rows)
     scale = 1.0 / math.sqrt(facet_rows)
-    for f, (mr, mi) in enumerate(tables):
-        mr, mi = mr.astype(BF16), mi.astype(BF16)
-        rows_ref[f] = block([[mr, -mi], [mi, mr]])
+    for f in range(facets):
         part = dot(rows_ref[f], pieces_ref[f].reshape(2 * facet_rows, CONTRIB)) * scale
         here = pl.ds(f * block_rows, block_rows)
         left_ref[here, :CONTRIB] = part[:block_rows].astype(BF16)
         left_ref[here, CONTRIB:] = part[block_rows:].astype(BF16)
-    shape = (facets, SUBGRID)
-    firsts = jnp.zeros(shape, jnp.int32)
-    for f in range(facets):
-        firsts = jnp.where(iota(shape, 0) == f, offsets_ref[1, f], firsts)
-    shift_real, shift_imag = cis(firsts * iota(shape, 1))
-    shape = (CONTRIB, SUBGRID)
-    tr, ti = cis(iota(shape, 0) * iota(shape, 1) * STEP)
-    weights = block([[tr, ti], [-ti, tr]]).astype(BF16)
+    weights = weights_ref[...]
+    shift_real, shift_imag = shift_ref[0], shift_ref[1]
     wide = dot(left_ref[...], weights)
     grid_real = jnp.zeros((block_rows, SUBGRID), F32)
     grid_imag = jnp.zeros((block_rows, SUBGRID), F32)
@@ -202,27 +225,14 @@
     own = (iota((LANES, LANES), 0) // PATCH) == (iota((LANES, LANES), 1) // PATCH)
     factor = 1.0 / math.sqrt(vis)
     for p in range(patch_rows):
-        strides = [cis(coords_ref[axis, p] * (8 * turn)) for axis in range(2)]
         for h in range(SIDE // group):
-            tables = []
-            for axis in range(2):
-                made = [
-                    patch_rows_of(
-                        coords_ref[axis, p, pl.ds(c, 1), :],
-                        (strides[axis][0][c : c + 1], strides[axis][1][c : c + 1]),
-                    )
-                    for c in range(h * group, (h + 1) * group)
-                ]
-                tables.append(
-                    tuple(jnp.concatenate([m[ri] for m in made], axis=0) for ri in range(2))
-                )
-            (ur, ui), (vr, vi) = tables
+            ur, ui = eu_ref[p, h, :LANES].astype(F32), eu_ref[p, h, LANES:].astype(F32)
             cells = (slice(p * PATCH, (p + 1) * PATCH), slice(h * LANES, (h + 1) * LANES))
             mr, mi = (
                 jnp.where(own, jnp.concatenate([grid[cells]] * group, axis=0), 0.0)
                 for grid in (grid_real, grid_imag)
             )
-            ev = jnp.concatenate([vr, vi], axis=0).astype(BF16)
+            ev = ev_ref[p, h]
             inner = dot(block([[mr, -mi], [mi, mr]]).astype(BF16), ev)
             ir, ii = times(ur, ui, inner[:LANES], inner[LANES:])
             wr, wi = [], []
@@ -336,15 +346,29 @@
     )
     own = exchange(transformed)
     other = swap(own)
+    patch_rows, vis = uv_coords.shape[1], uv_coords.shape[3]
+    halves = SIDE * PATCH // LANES
+    tables = call(
+        table_kernel,
+        "tables",
+        (subgrid_rows, offsets),
+        (uv_coords,),
+        (
+            shape((facets, 2 * block_rows, 2 * parts * rows), BF16),
+            shape((2 * CONTRIB, 2 * SUBGRID), BF16),
+            shape((2, facets, SUBGRID), F32),
+            shape((patch_rows, halves, 2 * LANES, vis), BF16),
+            shape((patch_rows, halves, 2 * LANES, vis), BF16),
+        ),
+    )
     keep, give, residual_vis = call(
         grid_kernel,
         "grid",
-        (subgrid_rows, offsets),
-        (own, other, uv_coords, observed),
+        (),
+        (own, other, *tables, observed),
         (pieces, pieces, shape(observed.shape, BF16)),
         (
             pltpu.VMEM((facets, 2, parts, rows, CONTRIB), BF16),
-            pltpu.VMEM((facets, 2 * block_rows, 2 * parts * rows), BF16),
             pltpu.VMEM((facets * block_rows, 2 * CONTRIB), BF16),
             pltpu.VMEM((2, block_rows, SUBGRID), F32),
             pltpu.VMEM((facets * block_rows, 2 * SUBGRID), BF16),

time: 45.4 us -> 44.7 us (0.985)
  waiting for transfers between devices: 2.95 us -> 1.16 us
  Pallas kernels: 7.31 us -> 7.78 us
    ppermute x2, waiting for transfers between devices: 2.95 us -> 1.16 us  [swap(): return lax.ppermute(value, 'freq', [(q, q ^ 1) for q in range(parts)])]
    pallas_call x3 -> x4, Pallas kernels: 7.31 us -> 7.78 us  [call(): pl.pallas_call(kernel, name=name, out_shape=outs, in_specs=[smem] * len(s...]
  transfers between devices with their start and end apart: 2 -> 2, of which waited for: 2 -> 1; matrix products, arithmetic and copies ran while one was open for 0% -> 0% of each run, Pallas kernels for 0% -> 5%
where the time goes in v2:
time: 44.7 us; the launch traced here: 44.4 us
  blocking collectives  31.7 us (71%)
  Pallas kernels  7.78 us (17%)
  local copies, waits for them, and re-layouts  1.73 us (4%)
  between operations  1.36 us (3%)
  waiting for transfers between devices  1.16 us (3%)
  starting transfers between devices  0.56 us (1%)
    all_to_all x2, blocking collectives, exchange(): lax.all_to_all(value, ('freq', 'facet'), split_axis=0, concat_axis=0, axi...  31.7 us
    pallas_call x4, Pallas kernels, call(): pl.pallas_call(kernel, name=name, out_shape=outs, in_specs=[smem] * len(s...  7.78 us
    unnamed x10, local copies, waits for them, and re-layouts  1.73 us
    ppermute x2, waiting for transfers between devices, swap(): return lax.ppermute(value, 'freq', [(q, q ^ 1) for q in range(parts)])  1.16 us
  transfers between devices with their start and end apart: 2, of which 1 were waited for; matrix products, arithmetic and copies ran while one was open for 0% of the time, Pallas kernels for 5%

profile of v2, /device:TPU:0, one launch (start us, length us, event | category | flops | bytes accessed | tf_op | source)
XLA Modules:
  0.0 44.4 jit_solution(16186729414288993248)
XLA Ops:
  1.3 0.0 copy-start.3
  1.3 0.7 %copy-done.3 = s32[8,2]{0,1:T(2,128)S(1)} copy-done((s32[8,2]{0,1:T(2,128)S(1)}, s32[8,2]{0,1:T(2,128)}, u32[]{:S(2)}) %copy-start.3) | copy-done | bytes 88
  2.0 0.0 copy-start
  2.0 1.0 %copy-done = bf16[1,2,32,4096]{3,2,1,0:T(8,128)(2,1)S(1)} copy-done((bf16[1,2,32,4096]{3,2,1,0:T(8,128)(2,1)S(1)}, bf16[1,2,32,4096]{3,2,1,0:T(8,128)(2,1)}, u32[]{:S(2)}) %copy-start) | copy-done | bytes 524312
  3.0 1.0 %column.1 = bf16[16,2,32,128]{3,2,1,0:T(8,128)(2,1)S(1)} custom-call(s32[1]{0:T(128)S(6)} %copy.8.column_ref, s32[2,8]{1,0:T(2,128)S(1)} %bitcast.1, bf16[1,2,32,4096]{3,2,1,0:T(8,128)(2,1)S(1)} %copy-done), custom_call_target="tpu_custom_call" | custom-call | tf_op jit(solution)/shard_map/column/pallas_call | solution.py:304
  4.0 0.0 copy-start.1
  4.0 0.0 copy-start.4
  4.0 18.1 %all_to_all.10.own_ref = bf16[16,2,32,128]{3,2,1,0:T(8,128)(2,1)S(1)} all-to-all(bf16[16,2,32,128]{3,2,1,0:T(8,128)(2,1)S(1)} %column.1), channel_id=1, replica_groups={{0,4,8,12,16,20,24,28,2,6,10,14,18,22,26,30},{1,5,9,13,17,21,25,29,3,7,..., dimensions={0} | all-to-all | bytes 524288 | tf_op jit(solution)/shard_map/all_to_all | solution.py:331
  22.2 0.0 copy-start.2
  22.2 0.0 collective-permute-start
  22.2 0.0 copy-done.1
  22.2 0.0 copy-done.4
  22.2 2.4 %tables.1 = (bf16[8,128,256]{2,1,0:T(8,128)(2,1)S(1)}, bf16[256,512]{1,0:T(8,128)(2,1)S(1)}, f32[2,8,256]{2,1,0:T(8,128)S(1)}, bf16[2,2,256,512]{3,2,1,0:T(8,128)(2,1)S(1)}, bf16[2,2,256,512]{3,2,1,0:T(8,128)(2,1)S(1)}) custom-call(s32[8]{0:T(128)S(1)} %copy-done.4, s32[2,8]{1,0:T(2,128)S(1)} %bitcast.2, s32[2,2,8,512]{3,2,1,0:T(8,128)S(1)} %copy-done.1), custom_call_target="tpu_custom_call" | custom-call | tf_op jit(solution)/shard_map/tables/pallas_call | solution.py:304
  24.6 0.0 collective-permute-done.other_ref
  24.6 0.0 copy-done.2
  24.6 2.4 %grid.1 = (bf16[16,2,32,128]{3,2,1,0:T(8,128)(2,1)S(1)}, bf16[16,2,32,128]{3,2,1,0:T(8,128)(2,1)S(1)}, bf16[2,2,8,512]{3,2,1,0:T(8,128)(2,1)}) custom-call(bf16[16,2,32,128]{3,2,1,0:T(8,128)(2,1)S(1)} %all_to_all.10.own_ref, bf16[16,2,32,128]{3,2,1,0:T(8,128)(2,1)S(1)} %collective-permute-done.other_ref, ...), custom_call_target="tpu_custom_call" | custom-call | tf_op jit(solution)/shard_map/grid/pallas_call | solution.py:304
  27.1 0.6 %collective-permute-start.1 = (bf16[16,2,32,128]{3,2,1,0:T(8,128)(2,1)S(1)}, bf16[16,2,32,128]{3,2,1,0:T(8,128)(2,1)S(1)}, u32[]{:S(2)}, u32[]{:S(2)}) collective-permute-start(bf16[16,2,32,128]{3,2,1,0:T(8,128)(2,1)S(1)} %get-tuple-element.16), channel_id=1, source_target_pairs={{0,1},{1,0},{2,3},{3,2},{4,5},{5,4},{6,7},{7,6},{8,9},{9,8},{10,11... | collective-permute-start | bytes 786440 | tf_op jit(solution)/shard_map/ppermute | solution.py:336
  27.7 1.2 %collective-permute-done.1 = bf16[16,2,32,128]{3,2,1,0:T(8,128)(2,1)S(1)} collective-permute-done((bf16[16,2,32,128]{3,2,1,0:T(8,128)(2,1)S(1)}, bf16[16,2,32,128]{3,2,1,0:T(8,128)(2,1)S(1)}, u32[]{:S(2)}, u32[]{:S(2)}) %collective-permute-start.1) | collective-permute-done | bytes 262176 | tf_op jit(solution)/shard_map/ppermute | solution.py:336
  28.8 0.1 add_convert_fusion
  28.9 13.6 %all_to_all.11.in_ref = bf16[16,2,32,128]{3,2,1,0:T(8,128)(2,1)S(1)} all-to-all(bf16[16,2,32,128]{3,2,1,0:T(8,128)(2,1)S(1)} %add_convert_fusion), channel_id=1, replica_groups={{0,4,8,12,16,20,24,28,2,6,10,14,18,22,26,30},{1,5,9,13,17,21,25,29,3,7,..., dimensions={0} | all-to-all | bytes 524288 | tf_op jit(solution)/shard_map/all_to_all | solution.py:331
  42.5 1.9 %image.1 = bf16[1,2,32,4096]{3,2,1,0:T(8,128)(2,1)} custom-call(s32[1]{0:T(128)S(6)} %copy.8.column_ref, s32[2,8]{1,0:T(2,128)S(1)} %bitcast.3, bf16[16,2,32,128]{3,2,1,0:T(8,128)(2,1)S(1)} %all_to_all.11.in_ref), custom_call_target="tpu_custom_call" | custom-call | tf_op jit(solution)/shard_map/image/pallas_call | solution.py:304
Async XLA Ops:
  1.3 0.7 %copy-start.3 = (s32[8,2]{0,1:T(2,128)S(1)}, s32[8,2]{0,1:T(2,128)}, u32[]{:S(2)}) copy-start(s32[8,2]{0,1:T(2,128)} %param.7) | copy-start | bytes 196
  2.0 1.0 %copy-start = (bf16[1,2,32,4096]{3,2,1,0:T(8,128)(2,1)S(1)}, bf16[1,2,32,4096]{3,2,1,0:T(8,128)(2,1)}, u32[]{:S(2)}) copy-start(bf16[1,2,32,4096]{3,2,1,0:T(8,128)(2,1)} %image_ref.1) | copy-start | bytes 1572868
  4.0 18.2 %copy-start.1 = (s32[2,2,8,512]{3,2,1,0:T(8,128)S(1)}, s32[2,2,8,512]{3,2,1,0:T(8,128)}, u32[]{:S(2)}) copy-start(s32[2,2,8,512]{3,2,1,0:T(8,128)} %coords_ref.1) | copy-start | bytes 196612
  4.0 18.2 %copy-start.4 = (s32[8]{0:T(128)S(1)}, s32[8]{0:T(128)}, u32[]{:S(2)}) copy-start(s32[8]{0:T(128)} %starts_ref.1) | copy-start | bytes 100
  22.2 2.5 %copy-start.2 = (bf16[2,2,8,512]{3,2,1,0:T(8,128)(2,1)S(1)}, bf16[2,2,8,512]{3,2,1,0:T(8,128)(2,1)}, u32[]{:S(2)}) copy-start(bf16[2,2,8,512]{3,2,1,0:T(8,128)(2,1)} %seen_ref.1) | copy-start | bytes 98308
  22.2 2.5 %collective-permute-start = (bf16[16,2,32,128]{3,2,1,0:T(8,128)(2,1)S(1)}, bf16[16,2,32,128]{3,2,1,0:T(8,128)(2,1)S(1)}, u32[]{:S(2)}, u32[]{:S(2)}) collective-permute-start(bf16[16,2,32,128]{3,2,1,0:T(8,128)(2,1)S(1)} %all_to_all.10.own_ref), channel_id=1, source_target_pairs={{0,1},{1,0},{2,3},{3,2},{4,5},{5,4},{6,7},{7,6},{8,9},{9,8},{10,11... | collective-permute-start | bytes 786440 | tf_op jit(solution)/shard_map/ppermute | solution.py:336
  27.1 1.7 %collective-permute-start.1 = (bf16[16,2,32,128]{3,2,1,0:T(8,128)(2,1)S(1)}, bf16[16,2,32,128]{3,2,1,0:T(8,128)(2,1)S(1)}, u32[]{:S(2)}, u32[]{:S(2)}) collective-permute-start(bf16[16,2,32,128]{3,2,1,0:T(8,128)(2,1)S(1)} %get-tuple-element.16), channel_id=1, source_target_pairs={{0,1},{1,0},{2,3},{3,2},{4,5},{5,4},{6,7},{7,6},{8,9},{9,8},{10,11... | collective-permute-start | bytes 786440 | tf_op jit(solution)/shard_map/ppermute | solution.py:336

commit v3 on v2

v3 whole, which is shorter than its diff:
```python
import functools
import math

import jax
import jax.numpy as jnp
from jax import lax
from jax.experimental import pallas as pl
from jax.experimental.pallas import tpu as pltpu
from jax.sharding import PartitionSpec as P

IMAGE = 32768
CONTRIB = 128
SUBGRID = 256
PATCH = 32
SIDE = 8
STEP = 128
PERIOD = 256
LANES = 128
MASK = IMAGE - 1

F32 = jnp.float32
BF16 = jnp.bfloat16


def iota(shape, axis):
    return lax.broadcasted_iota(jnp.int32, shape, axis)


def cis(turns):
    turns = turns & MASK
    quarter = (turns + IMAGE // 8) >> 13
    x = (turns - (quarter << 13)).astype(F32) * (2.0 * math.pi / IMAGE)
    x2 = x * x
    sine = x * (1.0 + x2 * (-1.0 / 6 + x2 * (1.0 / 120 - x2 * (1.0 / 5040))))
    cosine = 1.0 + x2 * (-0.5 + x2 * (1.0 / 24 + x2 * (-1.0 / 720 + x2 * (1.0 / 40320))))
    odd = (quarter & 1) == 1
    real = jnp.where(odd, sine, cosine)
    imag = jnp.where(odd, cosine, sine)
    real = jnp.where(((quarter + 1) & 2) == 2, -real, real)
    imag = jnp.where((quarter & 2) == 2, -imag, imag)
    return real, imag


def times(ar, ai, br, bi):
    return ar * br - ai * bi, ar * bi + ai * br


def times_conj(ar, ai, br, bi):
    return ar * br + ai * bi, ai * br - ar * bi


def block(rows):
    return jnp.concatenate([jnp.concatenate(row, axis=1) for row in rows], axis=0)


def dot(left, right):
    return lax.dot_general(left, right, (((1,), (0,)), ((), ())), preferred_element_type=F32)


def dot_t(left, right):
    return lax.dot_general(left, right, (((1,), (1,)), ((), ())), preferred_element_type=F32)


def dot_0(left, right):
    return lax.dot_general(left, right, (((0,), (0,)), ((), ())), preferred_element_type=F32)


def column_tables(column, first, extent):
    col_step = IMAGE // extent
    far_count = extent // LANES
    near = ((column + col_step * iota((LANES, CONTRIB), 1)) & MASK) * iota((LANES, CONTRIB), 0)
    shape = (far_count, CONTRIB)
    far = ((column + col_step * iota(shape, 1)) & MASK) * ((first + LANES * iota(shape, 0)) & MASK)
    return cis(-near), cis(-far)


def near_weights(near):
    real, imag = near
    return block([[real, imag], [-imag, real]]).astype(BF16)


CHUNK = 8
GROUP = LANES // PATCH


def cell_of(lane):
    half, inside = lane // LANES, lane % LANES
    return (half * GROUP + inside % GROUP) * PATCH + inside // GROUP


def column_kernel(
    column_ref,
    offsets_hbm,
    image_hbm,
    coords_hbm,
    seen_hbm,
    out_ref,
    near_ref,
    far_ref,
    weights_ref,
    coords_ref,
    seen_ref,
    left_ref,
    offsets_ref,
    small_sem,
    image_sem,
    later_sem,
):
    rows, extent = image_hbm.shape[2:]
    far_count = extent // LANES
    small = pltpu.make_async_copy(offsets_hbm, offsets_ref, small_sem)
    small.start()
    large = []
    for ri in range(2):
        copy = pltpu.make_async_copy(image_hbm.at[0, ri], left_ref.at[ri], image_sem.at[ri])
        copy.start()
        large.append(copy)
    later = [
        pltpu.make_async_copy(coords_hbm, coords_ref, later_sem.at[0]),
        pltpu.make_async_copy(seen_hbm, seen_ref, later_sem.at[1]),
    ]
    for copy in later:
        copy.start()
    for h in range(SUBGRID // LANES):
        shape = (CONTRIB, LANES)
        tr, ti = cis(iota(shape, 0) * cell_of(iota(shape, 1) + h * LANES) * STEP)
        weights_ref[:, 2 * h * LANES : 2 * (h + 1) * LANES] = block([[tr, ti], [-ti, tr]]).astype(BF16)
    small.wait()
    first = offsets_ref[1, lax.axis_index("facet")]
    near, far = column_tables(column_ref[0], first, extent)
    near_ref[...] = near_weights(near)
    far_ref[0], far_ref[1] = far
    real = jnp.zeros((rows, CONTRIB), F32)
    imag = jnp.zeros((rows, CONTRIB), F32)
    for copy in large:
        copy.wait()
    left = [
        jnp.concatenate([left_ref[ri, :, pl.ds(y1 * LANES, LANES)] for ri in range(2)], axis=1)
        for y1 in range(far_count)
    ]
    value = dot(jnp.concatenate(left, axis=0), near_ref[...])
    for y1 in range(far_count):
        part = value[y1 * rows : (y1 + 1) * rows]
        here = slice(y1, y1 + 1)
        pr, pi = times(part[:, :CONTRIB], part[:, CONTRIB:], far[0][here], far[1][here])
        real += pr
        imag += pi
    scale = 1.0 / math.sqrt(extent)
    both = jnp.stack([(real * scale).astype(BF16), (imag * scale).astype(BF16)])
    for member in range(out_ref.shape[0]):
        out_ref[member] = both
    for copy in later:
        copy.wait()


def row_tables(starts_ref, offsets_ref, facets, block_rows, facet_rows):
    half_step = IMAGE // facet_rows // 2
    owners = SUBGRID // block_rows
    index = lax.axis_index("freq") * lax.axis_size("facet") + lax.axis_index("facet")
    start = starts_ref[index // owners]
    shape = (block_rows, facet_rows)
    row = (index % owners) * block_rows + iota(shape, 0)
    half = (STEP // 2) * row - half_step * iota(shape, 1)
    top = cis(CONTRIB * half)[1]
    low = cis(half)[1]
    even = (half & (IMAGE // 2 - 1)) == 0
    limit = jnp.where((half & MASK) == 0, float(CONTRIB), -float(CONTRIB))
    kernel = jnp.where(even, limit, top / jnp.where(even, 1.0, low)) * (1.0 / math.sqrt(facet_rows))
    by_place = (facets, facet_rows)
    by_row = (block_rows, LANES)
    firsts = jnp.zeros(by_place, jnp.int32)
    lane_firsts = jnp.zeros(by_row, jnp.int32)
    for f in range(facets):
        firsts = jnp.where(iota(by_place, 0) == f, offsets_ref[0, f], firsts)
        lane_firsts = jnp.where(iota(by_row, 1) == f, offsets_ref[0, f], lane_firsts)
    place = firsts + iota(by_place, 1)
    place_real, place_imag = cis(
        -start * (place & MASK) - (CONTRIB - 1) * half_step * (place & (facet_rows - 1))
    )
    row_real, row_imag = cis(
        ((index % owners) * block_rows + iota(by_row, 0))
        * (lane_firsts + (CONTRIB - 1) * (STEP // 2))
    )
    tables = []
    for f in range(facets):
        shift = (facet_rows - offsets_ref[0, f] % facet_rows) % facet_rows
        rolled = pltpu.roll(kernel, shift, 1)
        real, imag = times(
            row_real[:, f : f + 1], row_imag[:, f : f + 1], place_real[f : f + 1], place_imag[f : f + 1]
        )
        tables.append((rolled * real, rolled * imag))
    return tables


def patch_powers(coords):
    twice = jnp.concatenate([coords, coords], axis=0)
    real, imag = cis(twice * (IMAGE // PERIOD))
    step = times(real, imag, real, imag)
    first = iota(twice.shape, 0) < GROUP
    power = jnp.where(first, 1.0, real), jnp.where(first, 0.0, imag)
    yield power
    for _ in range(PATCH // 2 - 1):
        power = times(*power, *step)
        yield power


def table_kernel(
    starts_hbm,
    offsets_hbm,
    coords_ref,
    rows_ref,
    shift_ref,
    eu_ref,
    ev_ref,
    starts_ref,
    offsets_ref,
    sem,
):
    small = [
        pltpu.make_async_copy(starts_hbm, starts_ref, sem.at[0]),
        pltpu.make_async_copy(offsets_hbm, offsets_ref, sem.at[1]),
    ]
    for copy in small:
        copy.start()
    facets = offsets_ref.shape[1]
    patch_rows = coords_ref.shape[1]
    block_rows = patch_rows * PATCH
    for p in range(patch_rows):
        for h in range(SIDE // GROUP):
            for axis, ref in enumerate((eu_ref, ev_ref)):
                coords = coords_ref[axis, p, pl.ds(h * GROUP, GROUP), :]
                for k, power in enumerate(patch_powers(coords)):
                    for ri in range(2):
                        here = pl.ds(ri * LANES + k * 2 * GROUP, 2 * GROUP)
                        ref[p, h, here, :] = power[ri].astype(ref.dtype)
    for copy in small:
        copy.wait()
    tables = row_tables(starts_ref, offsets_ref, facets, block_rows, rows_ref.shape[2] // 2)
    for f, (mr, mi) in enumerate(tables):
        mr, mi = mr.astype(BF16), mi.astype(BF16)
        rows_ref[f] = block([[mr, -mi], [mi, mr]])
    shape = (facets, SUBGRID)
    firsts = jnp.zeros(shape, jnp.int32)
    for f in range(facets):
        firsts = jnp.where(iota(shape, 0) == f, offsets_ref[1, f], firsts)
    for ri, value in enumerate(cis(firsts * cell_of(iota(shape, 1)))):
        shift_ref[ri] = value * (1.0 / CONTRIB)


def grid_kernel(
    own_ref,
    other_ref,
    rows_ref,
    weights_ref,
    shift_ref,
    eu_ref,
    ev_ref,
    seen_ref,
    keep_ref,
    give_ref,
    res_ref,
    pieces_ref,
    left_ref,
    grid_ref,
    back_ref,
    narrow_ref,
):
    facets = rows_ref.shape[0]
    pairs = own_ref.shape[0] // facets
    piece_rows = own_ref.shape[2]
    facet_rows = 2 * pairs * piece_rows
    patch_rows = seen_ref.shape[1]
    block_rows = patch_rows * PATCH
    vis = seen_ref.shape[3]
    core = lax.axis_index("freq") % 2
    for f in range(facets):
        for y in range(pairs):
            for ri in range(2):
                pieces_ref[f, ri, 2 * y + core] = own_ref[y * facets + f, ri]
                pieces_ref[f, ri, 2 * y + 1 - core] = other_ref[y * facets + f, ri]
    for f in range(facets):
        part = dot(rows_ref[f], pieces_ref[f].reshape(2 * facet_rows, CONTRIB))
        here = pl.ds(f * block_rows, block_rows)
        left_ref[here, :CONTRIB] = part[:block_rows].astype(BF16)
        left_ref[here, CONTRIB:] = part[block_rows:].astype(BF16)
    shift_real, shift_imag = shift_ref[0], shift_ref[1]
    halves = SUBGRID // LANES
    pair = 2 * GROUP
    tile = (pair, LANES)
    same = iota(tile, 0) % GROUP == iota(tile, 1) % GROUP
    upper, lower = same & (iota(tile, 0) < GROUP), same & (iota(tile, 0) >= GROUP)
    own = iota((LANES, LANES), 0) % GROUP == iota((LANES, LANES), 1) % GROUP
    pick = (iota((PATCH, LANES), 1) // GROUP == iota((PATCH, LANES), 0)).astype(F32).astype(BF16)

    def predicted(h):
        wide = dot(left_ref[...], weights_ref[:, 2 * h * LANES : 2 * (h + 1) * LANES])
        total = [jnp.zeros((block_rows, LANES), F32)] * 2
        for f in range(facets):
            part = wide[f * block_rows : (f + 1) * block_rows]
            lanes = slice(h * LANES, (h + 1) * LANES)
            made = times(
                part[:, :LANES], part[:, LANES:], shift_real[f : f + 1, lanes], shift_imag[f : f + 1, lanes]
            )
            total = [old + new for old, new in zip(total, made)]
        for ri in range(2):
            grid_ref[h, ri] = total[ri].astype(BF16).astype(F32)

    def degrid(p, h):
        spread = []
        for ri in range(2):
            tiles = []
            for r in range(p * PATCH, (p + 1) * PATCH, 2):
                one, two = grid_ref[h, ri, pl.ds(r, 1), :], grid_ref[h, ri, pl.ds(r + 1, 1), :]
                tiles.append(jnp.where(upper, one, jnp.where(lower, two, 0.0)))
            spread.append(jnp.concatenate(tiles, axis=0).astype(BF16))
        mr, mi = spread
        return dot(block([[mr, -mi], [mi, mr]]), ev_ref[p, h])

    def weigh(p, h, inner):
        sums = [jnp.zeros((pair, vis), F32)] * 2
        for k in range(0, LANES, pair):
            made = times(
                eu_ref[p, h, pl.ds(k, pair), :],
                eu_ref[p, h, pl.ds(LANES + k, pair), :],
                inner[k : k + pair],
                inner[LANES + k : LANES + k + pair],
            )
            sums = [total + value for total, value in zip(sums, made)]
        res = []
        for ri, value in enumerate(sums):
            model = (value + pltpu.roll(value, GROUP, 0)) * (1.0 / PATCH)
            seen = seen_ref[ri, p, pl.ds(h * GROUP, GROUP), :].astype(F32)
            rounded = (jnp.concatenate([seen, seen], axis=0) - model).astype(BF16)
            res_ref[ri, p, pl.ds(h * GROUP, GROUP), :] = rounded[:GROUP]
            res.append(rounded.astype(F32))
        weighted = [[], []]
        for k in range(0, LANES, pair):
            made = times_conj(
                *res, eu_ref[p, h, pl.ds(k, pair), :], eu_ref[p, h, pl.ds(LANES + k, pair), :]
            )
            for ri in range(2):
                weighted[ri].append(made[ri])
        return jnp.concatenate(weighted[0] + weighted[1], axis=0).astype(BF16)

    def regrid(p, h, back):
        both = [
            back[:LANES, :LANES] + back[LANES:, LANES:],
            back[LANES:, :LANES] - back[:LANES, LANES:],
        ]
        both = jnp.concatenate([jnp.where(own, value, 0.0) for value in both], axis=1)
        cells = dot(pick, both.astype(BF16))
        for ri in range(2):
            back_ref[h, ri, pl.ds(p * PATCH, PATCH), :] = cells[:, ri * LANES : (ri + 1) * LANES]

    def widen(h):
        for f in range(facets):
            lanes = slice(h * LANES, (h + 1) * LANES)
            made = times_conj(
                back_ref[h, 0], back_ref[h, 1], shift_real[f : f + 1, lanes], shift_imag[f : f + 1, lanes]
            )
            for ri in range(2):
                to = (2 * h + ri) * LANES
                narrow_ref[pl.ds(f * block_rows, block_rows), to : to + LANES] = made[ri].astype(BF16)

    tasks = [(p, h) for h in range(halves) for p in range(patch_rows)]
    inner, back = {}, {}
    for h in range(halves):
        predicted(h)
        for p in range(patch_rows):
            inner[p, h] = degrid(p, h)
    for at, task in enumerate(tasks):
        left = weigh(*task, inner.pop(task))
        back[task] = dot_t(left, ev_ref[task[0], task[1]])
        if at:
            regrid(*tasks[at - 1], back.pop(tasks[at - 1]))
    regrid(*tasks[-1], back.pop(tasks[-1]))
    for h in range(halves):
        widen(h)
    narrowed = dot_t(narrow_ref[...], weights_ref[...]).astype(BF16)
    for f in range(facets):
        part = narrowed[f * block_rows : (f + 1) * block_rows]
        part = jnp.concatenate([part[:, :CONTRIB], part[:, CONTRIB:]], axis=0)
        product = dot_0(rows_ref[f], part).astype(BF16)
        pieces_ref[f] = product.reshape(2, 2 * pairs, piece_rows, CONTRIB)
        for y in range(pairs):
            for ri in range(2):
                keep_ref[y * facets + f, ri] = pieces_ref[f, ri, 2 * y + core]
                give_ref[y * facets + f, ri] = pieces_ref[f, ri, 2 * y + 1 - core]


def image_kernel(scale, in_ref, near_ref, far_ref, out_hbm, stage_ref, sem):
    parts = in_ref.shape[0]
    rows, extent = out_hbm.shape[2:]
    far_count = extent // LANES
    real, imag = (
        sum(in_ref[q, ri].astype(F32) for q in range(parts)) * scale for ri in range(2)
    )
    copies = []
    for top in range(0, far_count, CHUNK):
        left = []
        for y1 in range(top, top + CHUNK):
            ar, ai = times_conj(real, imag, far_ref[0, y1 : y1 + 1], far_ref[1, y1 : y1 + 1])
            left.append(jnp.concatenate([ar, ai], axis=1).astype(BF16))
        value = dot_t(jnp.concatenate(left, axis=0), near_ref[...])
        value = (value * (1.0 / math.sqrt(CONTRIB))).astype(BF16)
        for y1 in range(CHUNK):
            for ri in range(2):
                stage_ref[ri, :, pl.ds((top + y1) * LANES, LANES)] = value[
                    y1 * rows : (y1 + 1) * rows, ri * LANES : (ri + 1) * LANES
                ]
        for ri in range(2):
            span = pl.ds(top * LANES, CHUNK * LANES)
            copy = pltpu.make_async_copy(
                stage_ref.at[ri, :, span], out_hbm.at[0, ri, :, span], sem.at[len(copies)]
            )
            copy.start()
            copies.append(copy)
    for copy in copies:
        copy.wait()


HBM = pl.BlockSpec(memory_space=pltpu.HBM)
SMEM = pl.BlockSpec(memory_space=pltpu.SMEM)
VMEM = pl.BlockSpec(memory_space=pltpu.VMEM)


def call(kernel, name, operands, in_specs, outs, scratch=(), out_specs=None):
    return pl.pallas_call(
        kernel,
        name=name,
        out_shape=outs,
        in_specs=in_specs,
        out_specs=out_specs or jax.tree.map(lambda _: VMEM, outs),
        scratch_shapes=list(scratch),
        compiler_params=pltpu.CompilerParams(vmem_limit_bytes=40 * 1024 * 1024),
    )(*operands)


def on_device(facet_image, facet_offsets, subgrid_rows, column_offset, uv_coords, observed):
    shape = jax.ShapeDtypeStruct
    rows, extent = facet_image.shape[2:]
    facets = lax.axis_size("facet")
    parts = lax.axis_size("freq")
    subgrids = subgrid_rows.shape[0]
    block_rows = uv_coords.shape[1] * PATCH
    members = facets * parts // 2
    groups = [
        [(2 * y + c) * facets + f for y in range(parts // 2) for f in range(facets)]
        for c in range(2)
    ]
    offsets = facet_offsets.T

    def exchange(value):
        return lax.all_to_all(
            value, ("freq", "facet"), split_axis=0, concat_axis=0, axis_index_groups=groups, tiled=True
        )

    def in_hbm(value):
        return pltpu.with_memory_space_constraint(value, pltpu.HBM)

    def swap(value):
        return lax.ppermute(value, "freq", [(q, q ^ 1) for q in range(parts)])

    pieces = shape((members, 2, rows, CONTRIB), BF16)
    far_count = extent // LANES
    transformed, near, far, weights, coords, seen = call(
        column_kernel,
        "column",
        (column_offset, *map(in_hbm, (offsets, facet_image, uv_coords, observed))),
        [SMEM] + [HBM] * 4,
        (
            pieces,
            shape((2 * LANES, 2 * CONTRIB), BF16),
            shape((2, far_count, CONTRIB), F32),
            shape((2 * CONTRIB, 2 * SUBGRID), BF16),
            shape(uv_coords.shape, jnp.int32),
            shape(observed.shape, BF16),
        ),
        (
            pltpu.VMEM(facet_image.shape[1:], BF16),
            pltpu.SMEM(offsets.shape, jnp.int32),
            pltpu.SemaphoreType.DMA,
            pltpu.SemaphoreType.DMA((2,)),
            pltpu.SemaphoreType.DMA((2,)),
        ),
    )
    own = exchange(transformed)
    other = swap(own)
    patch_rows, vis = uv_coords.shape[1], uv_coords.shape[3]
    halves = SIDE * PATCH // LANES
    row_products, *tables = call(
        table_kernel,
        "tables",
        (in_hbm(subgrid_rows), in_hbm(offsets), coords),
        [HBM, HBM, VMEM],
        (
            shape((facets, 2 * block_rows, 2 * parts * rows), BF16),
            shape((2, facets, SUBGRID), F32),
            shape((patch_rows, halves, 2 * LANES, vis), F32),
            shape((patch_rows, halves, 2 * LANES, vis), BF16),
        ),
        (
            pltpu.SMEM(subgrid_rows.shape, jnp.int32),
            pltpu.SMEM(offsets.shape, jnp.int32),
            pltpu.SemaphoreType.DMA((2,)),
        ),
    )
    keep, give, residual_vis = call(
        grid_kernel,
        "grid",
        (own, other, row_products, weights, *tables, seen),
        [VMEM] * 8,
        (pieces, pieces, shape(observed.shape, BF16)),
        (
            pltpu.VMEM((facets, 2, parts, rows, CONTRIB), BF16),
            pltpu.VMEM((facets * block_rows, 2 * CONTRIB), BF16),
            pltpu.VMEM((halves, 2, block_rows, LANES), F32),
            pltpu.VMEM((halves, 2, block_rows, LANES), F32),
            pltpu.VMEM((facets * block_rows, 2 * SUBGRID), BF16),
        ),
    )
    partial = (keep.astype(F32) + swap(give).astype(F32)).astype(BF16)
    shared_scale = 1.0 / CONTRIB / math.sqrt(parts * rows)
    scale = 1.0 / (math.sqrt(vis) * SUBGRID * math.sqrt(subgrids * CONTRIB) * shared_scale)
    image_residual = call(
        functools.partial(image_kernel, scale),
        "image",
        (exchange(partial), near, far),
        [VMEM] * 3,
        shape(facet_image.shape, BF16),
        (
            pltpu.VMEM(facet_image.shape[1:], BF16),
            pltpu.SemaphoreType.DMA((2 * far_count // CHUNK,)),
        ),
        HBM,
    )
    return (image_residual, residual_vis)


def solution(mesh):
    return jax.shard_map(
        on_device,
        mesh=mesh,
        in_specs=(
            P("facet", None, "freq", None),
            P(),
            P(),
            P(),
            P(None, ("freq", "facet"), None, None),
            P(None, ("freq", "facet"), None, None),
        ),
        out_specs=(P("facet", None, "freq", None), P(None, ("freq", "facet"), None, None)),
        check_vma=False,
    )
```

time: 44.7 us -> 41.5 us (0.928)
  local copies, waits for them, and re-layouts: 1.73 us -> 0 us
  Pallas kernels: 7.78 us -> 6.6 us
  waiting for transfers between devices: 1.16 us -> 1.8 us
    unnamed x10 -> x0, local copies, waits for them, and re-layouts: 1.73 us -> none
    pallas_call x4, Pallas kernels: 7.78 us -> 6.6 us  [call(): pl.pallas_call(kernel, name=name, out_shape=outs, in_specs=in_specs, out_...]
    ppermute x2, waiting for transfers between devices: 1.16 us -> 1.8 us  [swap(): return lax.ppermute(value, 'freq', [(q, q ^ 1) for q in range(parts)])]
  transfers between devices with their start and end apart: 2 -> 2, of which waited for: 1 -> 2; matrix products, arithmetic and copies ran while one was open for 0% -> 0% of each run, Pallas kernels for 5% -> 3%
where the time goes in v3:
time: 41.5 us; the launch traced here: 41.3 us
  blocking collectives  31.4 us (76%)
  Pallas kernels  6.6 us (16%)
  waiting for transfers between devices  1.8 us (4%)
  between operations  1.3 us (3%)
    all_to_all x2, blocking collectives, exchange(): lax.all_to_all(value, ('freq', 'facet'), split_axis=0, concat_axis=0, axi...  31.4 us
    pallas_call x4, Pallas kernels, call(): pl.pallas_call(kernel, name=name, out_shape=outs, in_specs=in_specs, out_...  6.6 us
    ppermute x2, waiting for transfers between devices, swap(): return lax.ppermute(value, 'freq', [(q, q ^ 1) for q in range(parts)])  1.8 us
  transfers between devices with their start and end apart: 2, of which 2 were waited for; matrix products, arithmetic and copies ran while one was open for 0% of the time, Pallas kernels for 3%

profile of v3, /device:TPU:0, one launch (start us, length us, event | category | flops | bytes accessed | tf_op | source)
XLA Modules:
  0.0 41.3 jit_solution(1305412648260840320)
XLA Ops:
  1.3 1.4 %column.1 = (bf16[16,2,32,128]{3,2,1,0:T(8,128)(2,1)S(1)}, bf16[256,256]{1,0:T(8,128)(2,1)S(1)}, f32[2,32,128]{2,1,0:T(8,128)S(1)}, bf16[256,512]{1,0:T(8,128)(2...) custom-call(s32[1]{0:T(128)S(6)} %copy.8.column_ref, s32[2,8]{1,0:T(2,128)} %bitcast.1, ...), custom_call_target="tpu_custom_call" | custom-call | tf_op jit(solution)/shard_map/column/pallas_call | solution.py:428
  2.7 18.0 %all_to_all.10.own_ref = bf16[16,2,32,128]{3,2,1,0:T(8,128)(2,1)S(1)} all-to-all(bf16[16,2,32,128]{3,2,1,0:T(8,128)(2,1)S(1)} %get-tuple-element.15), channel_id=1, replica_groups={{0,4,8,12,16,20,24,28,2,6,10,14,18,22,26,30},{1,5,9,13,17,21,25,29,3,7,..., dimensions={0} | all-to-all | bytes 524288 | tf_op jit(solution)/shard_map/all_to_all | solution.py:454
  20.7 0.0 collective-permute-start
  20.7 1.1 %tables.1 = (bf16[8,128,256]{2,1,0:T(8,128)(2,1)S(1)}, f32[2,8,256]{2,1,0:T(8,128)S(1)}, f32[2,2,256,512]{3,2,1,0:T(8,128)S(1)}, bf16[2,2,256,512]{3,2,1,0:T(8,128)(2,1)S(1)}) custom-call(s32[8]{0:T(128)} %starts_hbm.1, s32[2,8]{1,0:T(2,128)} %bitcast.2, s32[2,2,8,512]{3,2,1,0:T(8,128)S(1)} %get-tuple-element.16.coords_ref), custom_call_target="tpu_custom_call" | custom-call | tf_op jit(solution)/shard_map/tables/pallas_call | solution.py:428
  21.9 0.4 collective-permute-done.other_ref
  22.3 2.9 %grid.1 = (bf16[16,2,32,128]{3,2,1,0:T(8,128)(2,1)S(1)}, bf16[16,2,32,128]{3,2,1,0:T(8,128)(2,1)S(1)}, bf16[2,2,8,512]{3,2,1,0:T(8,128)(2,1)}) custom-call(bf16[16,2,32,128]{3,2,1,0:T(8,128)(2,1)S(1)} %all_to_all.10.own_ref, bf16[16,2,32,128]{3,2,1,0:T(8,128)(2,1)S(1)} %collective-permute-done.other_ref, ...), custom_call_target="tpu_custom_call" | custom-call | tf_op jit(solution)/shard_map/grid/pallas_call | solution.py:428
  25.2 0.1 collective-permute-start.1
  25.3 1.4 %collective-permute-done.1 = bf16[16,2,32,128]{3,2,1,0:T(8,128)(2,1)S(1)} collective-permute-done((bf16[16,2,32,128]{3,2,1,0:T(8,128)(2,1)S(1)}, bf16[16,2,32,128]{3,2,1,0:T(8,128)(2,1)S(1)}, u32[]{:S(2)}, u32[]{:S(2)}) %collective-permute-start.1) | collective-permute-done | bytes 262176 | tf_op jit(solution)/shard_map/ppermute | solution.py:462
  26.7 0.1 add_convert_fusion
  26.8 13.3 %all_to_all.11.in_ref = bf16[16,2,32,128]{3,2,1,0:T(8,128)(2,1)S(1)} all-to-all(bf16[16,2,32,128]{3,2,1,0:T(8,128)(2,1)S(1)} %add_convert_fusion), channel_id=1, replica_groups={{0,4,8,12,16,20,24,28,2,6,10,14,18,22,26,30},{1,5,9,13,17,21,25,29,3,7,..., dimensions={0} | all-to-all | bytes 524288 | tf_op jit(solution)/shard_map/all_to_all | solution.py:454
  40.1 1.1 %image.1 = bf16[1,2,32,4096]{3,2,1,0:T(8,128)(2,1)} custom-call(bf16[16,2,32,128]{3,2,1,0:T(8,128)(2,1)S(1)} %all_to_all.11.in_ref, bf16[256,256]{1,0:T(8,128)(2,1)S(1)} %get-tuple-element.25.near_ref, f32[2,32,128]{2,1,0:T(8,128)S(1)} %get-tuple-element.26.far_ref), custom_call_target="tpu_custom_call" | custom-call | tf_op jit(solution)/shard_map/image/pallas_call | solution.py:428
Async XLA Ops:
  20.7 1.5 %collective-permute-start = (bf16[16,2,32,128]{3,2,1,0:T(8,128)(2,1)S(1)}, bf16[16,2,32,128]{3,2,1,0:T(8,128)(2,1)S(1)}, u32[]{:S(2)}, u32[]{:S(2)}) collective-permute-start(bf16[16,2,32,128]{3,2,1,0:T(8,128)(2,1)S(1)} %all_to_all.10.own_ref), channel_id=1, source_target_pairs={{0,1},{1,0},{2,3},{3,2},{4,5},{5,4},{6,7},{7,6},{8,9},{9,8},{10,11... | collective-permute-start | bytes 786440 | tf_op jit(solution)/shard_map/ppermute | solution.py:462
  25.2 1.5 %collective-permute-start.1 = (bf16[16,2,32,128]{3,2,1,0:T(8,128)(2,1)S(1)}, bf16[16,2,32,128]{3,2,1,0:T(8,128)(2,1)S(1)}, u32[]{:S(2)}, u32[]{:S(2)}) collective-permute-start(bf16[16,2,32,128]{3,2,1,0:T(8,128)(2,1)S(1)} %get-tuple-element.24), channel_id=1, source_target_pairs={{0,1},{1,0},{2,3},{3,2},{4,5},{5,4},{6,7},{7,6},{8,9},{9,8},{10,11... | collective-permute-start | bytes 786440 | tf_op jit(solution)/shard_map/ppermute | solution.py:462

commit v4 on v3

--- a/solution.py
+++ b/solution.py
@@ -192,19 +192,15 @@
     return tables
 
 
-def patch_powers(coords):
+def patch_start(coords):
     twice = jnp.concatenate([coords, coords], axis=0)
     real, imag = cis(twice * (IMAGE // PERIOD))
-    step = times(real, imag, real, imag)
     first = iota(twice.shape, 0) < GROUP
-    power = jnp.where(first, 1.0, real), jnp.where(first, 0.0, imag)
-    yield power
-    for _ in range(PATCH // 2 - 1):
-        power = times(*power, *step)
-        yield power
+    return (jnp.where(first, 1.0, real), jnp.where(first, 0.0, imag)), times(real, imag, real, imag)
 
 
 def table_kernel(
+    piece_rows,
     starts_hbm,
     offsets_hbm,
     coords_ref,
@@ -214,6 +210,7 @@
     ev_ref,
     starts_ref,
     offsets_ref,
+    plain_ref,
     sem,
 ):
     small = [
@@ -227,18 +224,31 @@
     block_rows = patch_rows * PATCH
     for p in range(patch_rows):
         for h in range(SIDE // GROUP):
-            for axis, ref in enumerate((eu_ref, ev_ref)):
-                coords = coords_ref[axis, p, pl.ds(h * GROUP, GROUP), :]
-                for k, power in enumerate(patch_powers(coords)):
-                    for ri in range(2):
-                        here = pl.ds(ri * LANES + k * 2 * GROUP, 2 * GROUP)
-                        ref[p, h, here, :] = power[ri].astype(ref.dtype)
+            here = pl.ds(h * GROUP, GROUP)
+            start, step = patch_start(coords_ref[0, p, here, :])
+            for at, value in enumerate((*start, *step)):
+                eu_ref[p, h, at] = value
+            power, step = patch_start(coords_ref[1, p, here, :])
+            for k in range(PATCH // 2):
+                for ri in range(2):
+                    to = pl.ds(ri * LANES + k * 2 * GROUP, 2 * GROUP)
+                    ev_ref[p, h, to, :] = power[ri].astype(BF16)
+                power = times(*power, *step)
     for copy in small:
         copy.wait()
-    tables = row_tables(starts_ref, offsets_ref, facets, block_rows, rows_ref.shape[2] // 2)
+    facet_rows = rows_ref.shape[2]
+    tables = row_tables(starts_ref, offsets_ref, facets, block_rows, facet_rows)
     for f, (mr, mi) in enumerate(tables):
-        mr, mi = mr.astype(BF16), mi.astype(BF16)
-        rows_ref[f] = block([[mr, -mi], [mi, mr]])
+        plain_ref[f * 2 * block_rows : (2 * f + 1) * block_rows] = mr.astype(BF16)
+        plain_ref[(2 * f + 1) * block_rows : (f + 1) * 2 * block_rows] = mi.astype(BF16)
+    shape = (facet_rows, facet_rows)
+    half, inside = iota(shape, 1) // (facet_rows // 2), iota(shape, 1) % (facet_rows // 2)
+    core = (lax.axis_index("freq") + half) % 2
+    place = (2 * (inside // piece_rows) + core) * piece_rows + inside % piece_rows
+    order = (iota(shape, 0) == place).astype(F32).astype(BF16)
+    ordered = dot(plain_ref[...], order).astype(BF16)
+    for f in range(facets):
+        rows_ref[f] = ordered[f * 2 * block_rows : (f + 1) * 2 * block_rows]
     shape = (facets, SUBGRID)
     firsts = jnp.zeros(shape, jnp.int32)
     for f in range(facets):
@@ -256,33 +266,31 @@
     eu_ref,
     ev_ref,
     seen_ref,
-    keep_ref,
+    narrowed_ref,
     give_ref,
+    res_hbm,
     res_ref,
-    pieces_ref,
     left_ref,
     grid_ref,
     back_ref,
     narrow_ref,
+    res_sem,
 ):
     facets = rows_ref.shape[0]
     pairs = own_ref.shape[0] // facets
-    piece_rows = own_ref.shape[2]
-    facet_rows = 2 * pairs * piece_rows
     patch_rows = seen_ref.shape[1]
     block_rows = patch_rows * PATCH
     vis = seen_ref.shape[3]
-    core = lax.axis_index("freq") % 2
     for f in range(facets):
-        for y in range(pairs):
-            for ri in range(2):
-                pieces_ref[f, ri, 2 * y + core] = own_ref[y * facets + f, ri]
-                pieces_ref[f, ri, 2 * y + 1 - core] = other_ref[y * facets + f, ri]
-    for f in range(facets):
-        part = dot(rows_ref[f], pieces_ref[f].reshape(2 * facet_rows, CONTRIB))
-        here = pl.ds(f * block_rows, block_rows)
-        left_ref[here, :CONTRIB] = part[:block_rows].astype(BF16)
-        left_ref[here, CONTRIB:] = part[block_rows:].astype(BF16)
+        real, imag = (
+            jnp.concatenate(
+                [ref[y * facets + f, ri] for ref in (own_ref, other_ref) for y in range(pairs)], axis=0
+            )
+            for ri in range(2)
+        )
+        left = jnp.concatenate([rows_ref[f, :block_rows], rows_ref[f, block_rows:]], axis=1)
+        part = dot(left, block([[real, imag], [-imag, real]]))
+        left_ref[pl.ds(f * block_rows, block_rows), :] = part.astype(BF16)
     shift_real, shift_imag = shift_ref[0], shift_ref[1]
     halves = SUBGRID // LANES
     pair = 2 * GROUP
@@ -317,15 +325,14 @@
         return dot(block([[mr, -mi], [mi, mr]]), ev_ref[p, h])
 
     def weigh(p, h, inner):
-        sums = [jnp.zeros((pair, vis), F32)] * 2
-        for k in range(0, LANES, pair):
-            made = times(
-                eu_ref[p, h, pl.ds(k, pair), :],
-                eu_ref[p, h, pl.ds(LANES + k, pair), :],
-                inner[k : k + pair],
-                inner[LANES + k : LANES + k + pair],
-            )
-            sums = [total + value for total, value in zip(sums, made)]
+        start, step = [tuple(eu_ref[p, h, at + ri] for ri in range(2)) for at in (0, 2)]
+        rows_of = [
+            (inner[k : k + pair], inner[LANES + k : LANES + k + pair]) for k in range(0, LANES, pair)
+        ]
+        sums = rows_of[-1]
+        for new in rows_of[-2::-1]:
+            sums = [old + value for old, value in zip(times(*sums, *step), new)]
+        sums = times(*sums, *start)
         res = []
         for ri, value in enumerate(sums):
             model = (value + pltpu.roll(value, GROUP, 0)) * (1.0 / PATCH)
@@ -334,12 +341,11 @@
             res_ref[ri, p, pl.ds(h * GROUP, GROUP), :] = rounded[:GROUP]
             res.append(rounded.astype(F32))
         weighted = [[], []]
-        for k in range(0, LANES, pair):
-            made = times_conj(
-                *res, eu_ref[p, h, pl.ds(k, pair), :], eu_ref[p, h, pl.ds(LANES + k, pair), :]
-            )
+        res = times_conj(*res, *start)
+        for k in range(PATCH // 2):
             for ri in range(2):
-                weighted[ri].append(made[ri])
+                weighted[ri].append(res[ri])
+            res = times_conj(*res, *step)
         return jnp.concatenate(weighted[0] + weighted[1], axis=0).astype(BF16)
 
     def regrid(p, h, back):
@@ -368,24 +374,44 @@
         predicted(h)
         for p in range(patch_rows):
             inner[p, h] = degrid(p, h)
+    narrowed = []
+
+    def finish(task):
+        regrid(*task, back.pop(task))
+        p, h = task
+        if p == patch_rows - 1:
+            widen(h)
+            lanes = pl.ds(2 * h * LANES, 2 * LANES)
+            narrowed.append(dot_t(narrow_ref[:, lanes], weights_ref[:, lanes]))
+
     for at, task in enumerate(tasks):
         left = weigh(*task, inner.pop(task))
         back[task] = dot_t(left, ev_ref[task[0], task[1]])
         if at:
-            regrid(*tasks[at - 1], back.pop(tasks[at - 1]))
-    regrid(*tasks[-1], back.pop(tasks[-1]))
-    for h in range(halves):
-        widen(h)
-    narrowed = dot_t(narrow_ref[...], weights_ref[...]).astype(BF16)
+            finish(tasks[at - 1])
+    result = pltpu.make_async_copy(res_ref, res_hbm, res_sem)
+    result.start()
+    finish(tasks[-1])
+    narrowed_ref[...] = sum(narrowed).astype(BF16)
+    adjoint_rows(1, rows_ref, narrowed_ref, give_ref)
+    result.wait()
+
+
+def adjoint_rows(half, rows_ref, narrowed_ref, out_ref):
+    facets, height, facet_rows = rows_ref.shape
+    block_rows = height // 2
+    pairs = out_ref.shape[0] // facets
+    piece_rows = out_ref.shape[2]
     for f in range(facets):
-        part = narrowed[f * block_rows : (f + 1) * block_rows]
-        part = jnp.concatenate([part[:, :CONTRIB], part[:, CONTRIB:]], axis=0)
-        product = dot_0(rows_ref[f], part).astype(BF16)
-        pieces_ref[f] = product.reshape(2, 2 * pairs, piece_rows, CONTRIB)
+        here = pl.ds(f * block_rows, block_rows)
+        real, imag = narrowed_ref[here, :CONTRIB], narrowed_ref[here, CONTRIB:]
+        lanes = pl.ds(half * (facet_rows // 2), facet_rows // 2)
+        product = dot_0(rows_ref[f, :, lanes], block([[real, imag], [imag, -real]])).astype(BF16)
         for y in range(pairs):
             for ri in range(2):
-                keep_ref[y * facets + f, ri] = pieces_ref[f, ri, 2 * y + core]
-                give_ref[y * facets + f, ri] = pieces_ref[f, ri, 2 * y + 1 - core]
+                out_ref[y * facets + f, ri] = product[
+                    y * piece_rows : (y + 1) * piece_rows, ri * CONTRIB : (ri + 1) * CONTRIB
+                ]
 
 
 def image_kernel(scale, in_ref, near_ref, far_ref, out_hbm, stage_ref, sem):
@@ -489,35 +515,49 @@
     patch_rows, vis = uv_coords.shape[1], uv_coords.shape[3]
     halves = SIDE * PATCH // LANES
     row_products, *tables = call(
-        table_kernel,
+        functools.partial(table_kernel, rows),
         "tables",
         (in_hbm(subgrid_rows), in_hbm(offsets), coords),
         [HBM, HBM, VMEM],
         (
-            shape((facets, 2 * block_rows, 2 * parts * rows), BF16),
+            shape((facets, 2 * block_rows, parts * rows), BF16),
             shape((2, facets, SUBGRID), F32),
-            shape((patch_rows, halves, 2 * LANES, vis), F32),
+            shape((patch_rows, halves, 4, 2 * GROUP, vis), F32),
             shape((patch_rows, halves, 2 * LANES, vis), BF16),
         ),
         (
             pltpu.SMEM(subgrid_rows.shape, jnp.int32),
             pltpu.SMEM(offsets.shape, jnp.int32),
+            pltpu.VMEM((facets * 2 * block_rows, parts * rows), BF16),
             pltpu.SemaphoreType.DMA((2,)),
         ),
     )
-    keep, give, residual_vis = call(
+    narrowed, give, residual_vis = call(
         grid_kernel,
         "grid",
         (own, other, row_products, weights, *tables, seen),
         [VMEM] * 8,
-        (pieces, pieces, shape(observed.shape, BF16)),
-        (
-            pltpu.VMEM((facets, 2, parts, rows, CONTRIB), BF16),
+        (
+            shape((facets * block_rows, 2 * CONTRIB), BF16),
+            pieces,
+            shape(observed.shape, BF16),
+        ),
+        (
+            pltpu.VMEM(observed.shape, BF16),
             pltpu.VMEM((facets * block_rows, 2 * CONTRIB), BF16),
             pltpu.VMEM((halves, 2, block_rows, LANES), F32),
             pltpu.VMEM((halves, 2, block_rows, LANES), F32),
             pltpu.VMEM((facets * block_rows, 2 * SUBGRID), BF16),
-        ),
+            pltpu.SemaphoreType.DMA,
+        ),
+        (VMEM, VMEM, HBM),
+    )
+    keep = call(
+        functools.partial(adjoint_rows, 0),
+        "keep",
+        (row_products, narrowed),
+        [VMEM] * 2,
+        pieces,
     )
     partial = (keep.astype(F32) + swap(give).astype(F32)).astype(BF16)
     shared_scale = 1.0 / CONTRIB / math.sqrt(parts * rows)

time: 41.5 us -> 41.2 us (level)
  waiting for transfers between devices: 1.8 us -> 1.21 us
    ppermute x2, waiting for transfers between devices: 1.8 us -> 1.21 us  [swap(): return lax.ppermute(value, 'freq', [(q, q ^ 1) for q in range(parts)])]
    pallas_call x4 -> x5, Pallas kernels: 6.6 us -> 6.51 us  [call(): pl.pallas_call(kernel, name=name, out_shape=outs, in_specs=in_specs, out_...]
  transfers between devices with their start and end apart: 2 -> 2, of which waited for: 2 -> 2; matrix products, arithmetic and copies ran while one was open for 0% -> 0% of each run, Pallas kernels for 3% -> 4%
where the time goes in v4:
time: 41.2 us; the launch traced here: 41 us
  blocking collectives  31.5 us (76%)
  Pallas kernels  6.51 us (16%)
  between operations  1.32 us (3%)
  waiting for transfers between devices  1.21 us (3%)
    all_to_all x2, blocking collectives, exchange(): lax.all_to_all(value, ('freq', 'facet'), split_axis=0, concat_axis=0, axi...  31.5 us
    pallas_call x5, Pallas kernels, call(): pl.pallas_call(kernel, name=name, out_shape=outs, in_specs=in_specs, out_...  6.51 us
    ppermute x2, waiting for transfers between devices, swap(): return lax.ppermute(value, 'freq', [(q, q ^ 1) for q in range(parts)])  1.21 us
  transfers between devices with their start and end apart: 2, of which 2 were waited for; matrix products, arithmetic and copies ran while one was open for 0% of the time, Pallas kernels for 4%

profile of v4, /device:TPU:0, one launch (start us, length us, event | category | flops | bytes accessed | tf_op | source)
XLA Modules:
  0.0 41.0 jit_solution(15134251352411707187)
XLA Ops:
  1.3 1.4 %column.1 = (bf16[16,2,32,128]{3,2,1,0:T(8,128)(2,1)S(1)}, bf16[256,256]{1,0:T(8,128)(2,1)S(1)}, f32[2,32,128]{2,1,0:T(8,128)S(1)}, bf16[256,512]{1,0:T(8,128)(2...) custom-call(s32[1]{0:T(128)S(6)} %copy.8.column_ref, s32[2,8]{1,0:T(2,128)} %bitcast.1, ...), custom_call_target="tpu_custom_call" | custom-call | tf_op jit(solution)/shard_map/column/pallas_call | solution.py:454
  2.7 18.0 %all_to_all.10.own_ref = bf16[16,2,32,128]{3,2,1,0:T(8,128)(2,1)S(1)} all-to-all(bf16[16,2,32,128]{3,2,1,0:T(8,128)(2,1)S(1)} %get-tuple-element.17), channel_id=1, replica_groups={{0,4,8,12,16,20,24,28,2,6,10,14,18,22,26,30},{1,5,9,13,17,21,25,29,3,7,..., dimensions={0} | all-to-all | bytes 524288 | tf_op jit(solution)/shard_map/all_to_all | solution.py:480
  20.7 0.0 collective-permute-start
  20.7 1.3 %tables.1 = (bf16[8,128,128]{2,1,0:T(8,128)(2,1)S(1)}, f32[2,8,256]{2,1,0:T(8,128)S(1)}, f32[2,2,4,8,512]{4,3,2,1,0:T(8,128)S(1)}, bf16[2,2,256,512]{3,2,1,0:T(8,128)(2,1)S(1)}) custom-call(s32[8]{0:T(128)} %starts_hbm.1, s32[2,8]{1,0:T(2,128)} %bitcast.2, s32[2,2,8,512]{3,2,1,0:T(8,128)S(1)} %get-tuple-element.15.coords_ref), custom_call_target="tpu_custom_call" | custom-call | tf_op jit(solution)/shard_map/tables/pallas_call | solution.py:454
  22.1 0.2 collective-permute-done.other_ref
  22.3 2.4 %grid.1 = (bf16[512,256]{1,0:T(8,128)(2,1)S(1)}, bf16[16,2,32,128]{3,2,1,0:T(8,128)(2,1)S(1)}, bf16[2,2,8,512]{3,2,1,0:T(8,128)(2,1)}) custom-call(bf16[16,2,32,128]{3,2,1,0:T(8,128)(2,1)S(1)} %all_to_all.10.own_ref, bf16[16,2,32,128]{3,2,1,0:T(8,128)(2,1)S(1)} %collective-permute-done.other_ref, bf16[8,128,128]{2,1,0:T(8,128)(2,1)S(1)} %get-tuple-element.16.rows_ref, ...), custom_call_target="tpu_custom_call" | custom-call | tf_op jit(solution)/shard_map/grid/pallas_call | solution.py:454
  24.7 0.4 collective-permute-start.1
  25.0 0.3 keep.1
  25.3 1.0 %collective-permute-done.1 = bf16[16,2,32,128]{3,2,1,0:T(8,128)(2,1)S(1)} collective-permute-done((bf16[16,2,32,128]{3,2,1,0:T(8,128)(2,1)S(1)}, bf16[16,2,32,128]{3,2,1,0:T(8,128)(2,1)S(1)}, u32[]{:S(2)}, u32[]{:S(2)}) %collective-permute-start.1) | collective-permute-done | bytes 262176 | tf_op jit(solution)/shard_map/ppermute | solution.py:488
  26.3 0.1 add_convert_fusion
  26.3 13.5 %all_to_all.11.in_ref = bf16[16,2,32,128]{3,2,1,0:T(8,128)(2,1)S(1)} all-to-all(bf16[16,2,32,128]{3,2,1,0:T(8,128)(2,1)S(1)} %add_convert_fusion), channel_id=1, replica_groups={{0,4,8,12,16,20,24,28,2,6,10,14,18,22,26,30},{1,5,9,13,17,21,25,29,3,7,..., dimensions={0} | all-to-all | bytes 524288 | tf_op jit(solution)/shard_map/all_to_all | solution.py:480
  39.8 1.1 %image.1 = bf16[1,2,32,4096]{3,2,1,0:T(8,128)(2,1)} custom-call(bf16[16,2,32,128]{3,2,1,0:T(8,128)(2,1)S(1)} %all_to_all.11.in_ref, bf16[256,256]{1,0:T(8,128)(2,1)S(1)} %get-tuple-element.25.near_ref, f32[2,32,128]{2,1,0:T(8,128)S(1)} %get-tuple-element.26.far_ref), custom_call_target="tpu_custom_call" | custom-call | tf_op jit(solution)/shard_map/image/pallas_call | solution.py:454
Async XLA Ops:
  20.7 1.5 %collective-permute-start = (bf16[16,2,32,128]{3,2,1,0:T(8,128)(2,1)S(1)}, bf16[16,2,32,128]{3,2,1,0:T(8,128)(2,1)S(1)}, u32[]{:S(2)}, u32[]{:S(2)}) collective-permute-start(bf16[16,2,32,128]{3,2,1,0:T(8,128)(2,1)S(1)} %all_to_all.10.own_ref), channel_id=1, source_target_pairs={{0,1},{1,0},{2,3},{3,2},{4,5},{5,4},{6,7},{7,6},{8,9},{9,8},{10,11... | collective-permute-start | bytes 786440 | tf_op jit(solution)/shard_map/ppermute | solution.py:488
  24.7 1.6 %collective-permute-start.1 = (bf16[16,2,32,128]{3,2,1,0:T(8,128)(2,1)S(1)}, bf16[16,2,32,128]{3,2,1,0:T(8,128)(2,1)S(1)}, u32[]{:S(2)}, u32[]{:S(2)}) collective-permute-start(bf16[16,2,32,128]{3,2,1,0:T(8,128)(2,1)S(1)} %get-tuple-element.24), channel_id=1, source_target_pairs={{0,1},{1,0},{2,3},{3,2},{4,5},{5,4},{6,7},{7,6},{8,9},{9,8},{10,11... | collective-permute-start | bytes 786440 | tf_op jit(solution)/shard_map/ppermute | solution.py:488

commit v5 on v4

--- a/solution.py
+++ b/solution.py
@@ -153,13 +153,19 @@
         copy.wait()
 
 
+def row_of(position):
+    inside = position % PATCH
+    half = PATCH // 2
+    return position - inside + jnp.where(inside < half, half - 1 - inside, inside)
+
+
 def row_tables(starts_ref, offsets_ref, facets, block_rows, facet_rows):
     half_step = IMAGE // facet_rows // 2
     owners = SUBGRID // block_rows
     index = lax.axis_index("freq") * lax.axis_size("facet") + lax.axis_index("facet")
     start = starts_ref[index // owners]
     shape = (block_rows, facet_rows)
-    row = (index % owners) * block_rows + iota(shape, 0)
+    row = (index % owners) * block_rows + row_of(iota(shape, 0))
     half = (STEP // 2) * row - half_step * iota(shape, 1)
     top = cis(CONTRIB * half)[1]
     low = cis(half)[1]
@@ -178,7 +184,7 @@
         -start * (place & MASK) - (CONTRIB - 1) * half_step * (place & (facet_rows - 1))
     )
     row_real, row_imag = cis(
-        ((index % owners) * block_rows + iota(by_row, 0))
+        ((index % owners) * block_rows + row_of(iota(by_row, 0)))
         * (lane_firsts + (CONTRIB - 1) * (STEP // 2))
     )
     tables = []
@@ -206,7 +212,8 @@
     coords_ref,
     rows_ref,
     shift_ref,
-    eu_ref,
+    wave_ref,
+    centre_ref,
     ev_ref,
     starts_ref,
     offsets_ref,
@@ -225,9 +232,15 @@
     for p in range(patch_rows):
         for h in range(SIDE // GROUP):
             here = pl.ds(h * GROUP, GROUP)
-            start, step = patch_start(coords_ref[0, p, here, :])
-            for at, value in enumerate((*start, *step)):
-                eu_ref[p, h, at] = value
+            twice = jnp.concatenate([coords_ref[0, p, here, :]] * 2, axis=0)
+            odd = jnp.where(iota(twice.shape, 0) < GROUP, 1, 3)
+            half_turn = IMAGE // PERIOD // 2
+            centre_ref[p, h, 0], centre_ref[p, h, 1] = cis(twice * ((PATCH - 1) * half_turn))
+            power, step = cis(twice * odd * half_turn), cis(twice * (4 * half_turn))
+            for k in range(PATCH // 4):
+                for ri in range(2):
+                    wave_ref[p, h, ri, pl.ds(k * 2 * GROUP, 2 * GROUP), :] = power[ri]
+                power = times(*power, *step)
             power, step = patch_start(coords_ref[1, p, here, :])
             for k in range(PATCH // 2):
                 for ri in range(2):
@@ -236,7 +249,7 @@
                 power = times(*power, *step)
     for copy in small:
         copy.wait()
-    facet_rows = rows_ref.shape[2]
+    facet_rows = rows_ref.shape[2] // 2
     tables = row_tables(starts_ref, offsets_ref, facets, block_rows, facet_rows)
     for f, (mr, mi) in enumerate(tables):
         plain_ref[f * 2 * block_rows : (2 * f + 1) * block_rows] = mr.astype(BF16)
@@ -248,7 +261,10 @@
     order = (iota(shape, 0) == place).astype(F32).astype(BF16)
     ordered = dot(plain_ref[...], order).astype(BF16)
     for f in range(facets):
-        rows_ref[f] = ordered[f * 2 * block_rows : (f + 1) * 2 * block_rows]
+        here = ordered[f * 2 * block_rows : (f + 1) * 2 * block_rows]
+        rows_ref[f, :, :facet_rows] = here
+        rows_ref[f, :block_rows, facet_rows:] = -here[block_rows:]
+        rows_ref[f, block_rows:, facet_rows:] = here[:block_rows]
     shape = (facets, SUBGRID)
     firsts = jnp.zeros(shape, jnp.int32)
     for f in range(facets):
@@ -263,7 +279,8 @@
     rows_ref,
     weights_ref,
     shift_ref,
-    eu_ref,
+    wave_ref,
+    centre_ref,
     ev_ref,
     seen_ref,
     narrowed_ref,
@@ -273,6 +290,7 @@
     left_ref,
     grid_ref,
     back_ref,
+    both_ref,
     narrow_ref,
     res_sem,
 ):
@@ -282,23 +300,20 @@
     block_rows = patch_rows * PATCH
     vis = seen_ref.shape[3]
     for f in range(facets):
-        real, imag = (
-            jnp.concatenate(
-                [ref[y * facets + f, ri] for ref in (own_ref, other_ref) for y in range(pairs)], axis=0
-            )
-            for ri in range(2)
-        )
-        left = jnp.concatenate([rows_ref[f, :block_rows], rows_ref[f, block_rows:]], axis=1)
-        part = dot(left, block([[real, imag], [-imag, real]]))
-        left_ref[pl.ds(f * block_rows, block_rows), :] = part.astype(BF16)
+        right = [
+            ref[y * facets + f, ri] for ri in range(2) for ref in (own_ref, other_ref) for y in range(pairs)
+        ]
+        part = dot(rows_ref[f], jnp.concatenate(right, axis=0)).astype(BF16)
+        for ri in range(2):
+            to = (pl.ds(f * block_rows, block_rows), pl.ds(ri * CONTRIB, CONTRIB))
+            left_ref[to] = part[ri * block_rows : (ri + 1) * block_rows]
     shift_real, shift_imag = shift_ref[0], shift_ref[1]
     halves = SUBGRID // LANES
     pair = 2 * GROUP
     tile = (pair, LANES)
     same = iota(tile, 0) % GROUP == iota(tile, 1) % GROUP
     upper, lower = same & (iota(tile, 0) < GROUP), same & (iota(tile, 0) >= GROUP)
-    own = iota((LANES, LANES), 0) % GROUP == iota((LANES, LANES), 1) % GROUP
-    pick = (iota((PATCH, LANES), 1) // GROUP == iota((PATCH, LANES), 0)).astype(F32).astype(BF16)
+    own = iota((PATCH, LANES), 1) % GROUP
 
     def predicted(h):
         wide = dot(left_ref[...], weights_ref[:, 2 * h * LANES : 2 * (h + 1) * LANES])
@@ -314,49 +329,61 @@
             grid_ref[h, ri] = total[ri].astype(BF16).astype(F32)
 
     def degrid(p, h):
-        spread = []
+        middle = PATCH // 2
+        made = []
         for ri in range(2):
-            tiles = []
-            for r in range(p * PATCH, (p + 1) * PATCH, 2):
-                one, two = grid_ref[h, ri, pl.ds(r, 1), :], grid_ref[h, ri, pl.ds(r + 1, 1), :]
-                tiles.append(jnp.where(upper, one, jnp.where(lower, two, 0.0)))
-            spread.append(jnp.concatenate(tiles, axis=0).astype(BF16))
-        mr, mi = spread
-        return dot(block([[mr, -mi], [mi, mr]]), ev_ref[p, h])
+            sums, differences = [], []
+            for k in range(0, middle, 2):
+                after, before = (
+                    [grid_ref[h, ri, pl.ds(p * PATCH + at + k + i, 1), :] for i in range(2)]
+                    for at in (middle, 0)
+                )
+                add = [one + two for one, two in zip(after, before)]
+                take = [one - two for one, two in zip(after, before)]
+                for tiles, (one, two) in ((sums, add), (differences, take)):
+                    tiles.append(jnp.where(upper, one, jnp.where(lower, two, 0.0)))
+            made.append([jnp.concatenate(tiles, axis=0).astype(BF16) for tiles in (sums, differences)])
+        (sr, dr), (si, di) = made
+        return dot(block([[sr, -si], [si, sr], [dr, -di], [di, dr]]), ev_ref[p, h])
 
     def weigh(p, h, inner):
-        start, step = [tuple(eu_ref[p, h, at + ri] for ri in range(2)) for at in (0, 2)]
-        rows_of = [
-            (inner[k : k + pair], inner[LANES + k : LANES + k + pair]) for k in range(0, LANES, pair)
-        ]
-        sums = rows_of[-1]
-        for new in rows_of[-2::-1]:
-            sums = [old + value for old, value in zip(times(*sums, *step), new)]
-        sums = times(*sums, *start)
+        height = LANES // 2
+        sums = [jnp.zeros((pair, vis), F32)] * 2
+        for k in range(0, height, pair):
+            cosine, sine = (wave_ref[p, h, ri, pl.ds(k, pair), :] for ri in range(2))
+            sr, si, dr, di = (inner[at + k : at + k + pair] for at in range(0, 4 * height, height))
+            sums = [sums[0] + (cosine * sr - sine * di), sums[1] + (cosine * si + sine * dr)]
+        centre = centre_ref[p, h, 0], centre_ref[p, h, 1]
+        sums = times(*(value + pltpu.roll(value, GROUP, 0) for value in sums), *centre)
         res = []
         for ri, value in enumerate(sums):
-            model = (value + pltpu.roll(value, GROUP, 0)) * (1.0 / PATCH)
+            model = value * (1.0 / PATCH)
             seen = seen_ref[ri, p, pl.ds(h * GROUP, GROUP), :].astype(F32)
             rounded = (jnp.concatenate([seen, seen], axis=0) - model).astype(BF16)
             res_ref[ri, p, pl.ds(h * GROUP, GROUP), :] = rounded[:GROUP]
             res.append(rounded.astype(F32))
-        weighted = [[], []]
-        res = times_conj(*res, *start)
-        for k in range(PATCH // 2):
-            for ri in range(2):
-                weighted[ri].append(res[ri])
-            res = times_conj(*res, *step)
-        return jnp.concatenate(weighted[0] + weighted[1], axis=0).astype(BF16)
+        res = times_conj(*res, *centre)
+        weighted = [
+            wave_ref[p, h, wave, pl.ds(k, pair), :] * res[ri]
+            for wave in range(2)
+            for ri in range(2)
+            for k in range(0, height, pair)
+        ]
+        return jnp.concatenate(weighted, axis=0).astype(BF16)
 
     def regrid(p, h, back):
-        both = [
-            back[:LANES, :LANES] + back[LANES:, LANES:],
-            back[LANES:, :LANES] - back[:LANES, LANES:],
-        ]
-        both = jnp.concatenate([jnp.where(own, value, 0.0) for value in both], axis=1)
-        cells = dot(pick, both.astype(BF16))
+        height = LANES // 2
+        quarters = [back[at : at + height] for at in range(0, 4 * height, height)]
+        near, far = [part[:, :LANES] for part in quarters], [part[:, LANES:] for part in quarters]
+        ar, ai = near[0] + far[1], near[1] - far[0]
+        br, bi = near[2] + far[3], near[3] - far[2]
+        both_ref[p, h, 0, :height], both_ref[p, h, 0, height:] = ar - bi, ar + bi
+        both_ref[p, h, 1, :height], both_ref[p, h, 1, height:] = ai + br, ai - br
         for ri in range(2):
-            back_ref[h, ri, pl.ds(p * PATCH, PATCH), :] = cells[:, ri * LANES : (ri + 1) * LANES]
+            cells = both_ref[p, h, ri, pl.ds(0, PATCH, stride=GROUP), :]
+            for c in range(1, GROUP):
+                cells = jnp.where(own == c, both_ref[p, h, ri, pl.ds(c, PATCH, stride=GROUP), :], cells)
+            back_ref[h, ri, pl.ds(p * PATCH, PATCH), :] = cells.astype(BF16).astype(F32)
 
     def widen(h):
         for f in range(facets):
@@ -398,7 +425,7 @@
 
 
 def adjoint_rows(half, rows_ref, narrowed_ref, out_ref):
-    facets, height, facet_rows = rows_ref.shape
+    facets, height, facet_rows = rows_ref.shape[0], rows_ref.shape[1], rows_ref.shape[2] // 2
     block_rows = height // 2
     pairs = out_ref.shape[0] // facets
     piece_rows = out_ref.shape[2]
@@ -520,9 +547,10 @@
         (in_hbm(subgrid_rows), in_hbm(offsets), coords),
         [HBM, HBM, VMEM],
         (
-            shape((facets, 2 * block_rows, parts * rows), BF16),
+            shape((facets, 2 * block_rows, 2 * parts * rows), BF16),
             shape((2, facets, SUBGRID), F32),
-            shape((patch_rows, halves, 4, 2 * GROUP, vis), F32),
+            shape((patch_rows, halves, 2, LANES // 2, vis), F32),
+            shape((patch_rows, halves, 2, 2 * GROUP, vis), F32),
             shape((patch_rows, halves, 2 * LANES, vis), BF16),
         ),
         (
@@ -536,7 +564,7 @@
         grid_kernel,
         "grid",
         (own, other, row_products, weights, *tables, seen),
-        [VMEM] * 8,
+        [VMEM] * 9,
         (
             shape((facets * block_rows, 2 * CONTRIB), BF16),
             pieces,
@@ -547,6 +575,7 @@
             pltpu.VMEM((facets * block_rows, 2 * CONTRIB), BF16),
             pltpu.VMEM((halves, 2, block_rows, LANES), F32),
             pltpu.VMEM((halves, 2, block_rows, LANES), F32),
+            pltpu.VMEM((patch_rows, halves, 2, LANES, LANES), F32),
             pltpu.VMEM((facets * block_rows, 2 * SUBGRID), BF16),
             pltpu.SemaphoreType.DMA,
         ),

time: 41.2 us -> 40.9 us (level)
  no operation moved by 1% of the time
where the time goes in v5:
time: 40.9 us; the launch traced here: 40.7 us
  blocking collectives  31.5 us (77%)
  Pallas kernels  6.23 us (15%)
  between operations  1.32 us (3%)
  waiting for transfers between devices  1.19 us (3%)
    all_to_all x2, blocking collectives, exchange(): lax.all_to_all(value, ('freq', 'facet'), split_axis=0, concat_axis=0, axi...  31.5 us
    pallas_call x5, Pallas kernels, call(): pl.pallas_call(kernel, name=name, out_shape=outs, in_specs=in_specs, out_...  6.23 us
    ppermute x2, waiting for transfers between devices, swap(): return lax.ppermute(value, 'freq', [(q, q ^ 1) for q in range(parts)])  1.19 us
  transfers between devices with their start and end apart: 2, of which 2 were waited for; matrix products, arithmetic and copies ran while one was open for 0% of the time, Pallas kernels for 4%

profile of v5, /device:TPU:0, one launch (start us, length us, event | category | flops | bytes accessed | tf_op | source)
XLA Modules:
  0.0 40.7 jit_solution(3481706048927463540)
XLA Ops:
  1.3 1.4 %column.1 = (bf16[16,2,32,128]{3,2,1,0:T(8,128)(2,1)S(1)}, bf16[256,256]{1,0:T(8,128)(2,1)S(1)}, f32[2,32,128]{2,1,0:T(8,128)S(1)}, bf16[256,512]{1,0:T(8,128)(2...) custom-call(s32[1]{0:T(128)S(6)} %copy.8.column_ref, s32[2,8]{1,0:T(2,128)} %bitcast.1, ...), custom_call_target="tpu_custom_call" | custom-call | tf_op jit(solution)/shard_map/column/pallas_call | solution.py:481
  2.7 18.0 %all_to_all.10.own_ref = bf16[16,2,32,128]{3,2,1,0:T(8,128)(2,1)S(1)} all-to-all(bf16[16,2,32,128]{3,2,1,0:T(8,128)(2,1)S(1)} %get-tuple-element.18), channel_id=1, replica_groups={{0,4,8,12,16,20,24,28,2,6,10,14,18,22,26,30},{1,5,9,13,17,21,25,29,3,7,..., dimensions={0} | all-to-all | bytes 524288 | tf_op jit(solution)/shard_map/all_to_all | solution.py:507
  20.7 0.0 collective-permute-start
  20.7 1.3 %tables.1 = (bf16[8,128,256]{2,1,0:T(8,128)(2,1)S(1)}, f32[2,8,256]{2,1,0:T(8,128)S(1)}, f32[2,2,2,64,512]{4,3,2,1,0:T(8,128)S(1)}, f32[2,2,2,8,512]{4,3,2,1,0:T(8,128)S(1)}, bf16[2,2,256,512]{3,2,1,0:T(8,128)(2,1)S(1)}) custom-call(s32[8]{0:T(128)} %starts_hbm.1, s32[2,8]{1,0:T(2,128)} %bitcast.2, s32[2,2,8,512]{3,2,1,0:T(8,128)S(1)} %get-tuple-element.16.coords_ref), custom_call_target="tpu_custom_call" | custom-call | tf_op jit(solution)/shard_map/tables/pallas_call | solution.py:481
  22.1 0.2 collective-permute-done.other_ref
  22.3 2.1 %grid.1 = (bf16[512,256]{1,0:T(8,128)(2,1)S(1)}, bf16[16,2,32,128]{3,2,1,0:T(8,128)(2,1)S(1)}, bf16[2,2,8,512]{3,2,1,0:T(8,128)(2,1)}) custom-call(bf16[16,2,32,128]{3,2,1,0:T(8,128)(2,1)S(1)} %all_to_all.10.own_ref, bf16[16,2,32,128]{3,2,1,0:T(8,128)(2,1)S(1)} %collective-permute-done.other_ref, bf16[8,128,256]{2,1,0:T(8,128)(2,1)S(1)} %get-tuple-element.17.rows_ref, ...), custom_call_target="tpu_custom_call" | custom-call | tf_op jit(solution)/shard_map/grid/pallas_call | solution.py:481
  24.4 0.4 collective-permute-start.1
  24.7 0.3 keep.1
  25.0 1.0 %collective-permute-done.1 = bf16[16,2,32,128]{3,2,1,0:T(8,128)(2,1)S(1)} collective-permute-done((bf16[16,2,32,128]{3,2,1,0:T(8,128)(2,1)S(1)}, bf16[16,2,32,128]{3,2,1,0:T(8,128)(2,1)S(1)}, u32[]{:S(2)}, u32[]{:S(2)}) %collective-permute-start.1) | collective-permute-done | bytes 262176 | tf_op jit(solution)/shard_map/ppermute | solution.py:515
  26.0 0.1 add_convert_fusion
  26.1 13.5 %all_to_all.11.in_ref = bf16[16,2,32,128]{3,2,1,0:T(8,128)(2,1)S(1)} all-to-all(bf16[16,2,32,128]{3,2,1,0:T(8,128)(2,1)S(1)} %add_convert_fusion), channel_id=1, replica_groups={{0,4,8,12,16,20,24,28,2,6,10,14,18,22,26,30},{1,5,9,13,17,21,25,29,3,7,..., dimensions={0} | all-to-all | bytes 524288 | tf_op jit(solution)/shard_map/all_to_all | solution.py:507
  39.6 1.1 %image.1 = bf16[1,2,32,4096]{3,2,1,0:T(8,128)(2,1)} custom-call(bf16[16,2,32,128]{3,2,1,0:T(8,128)(2,1)S(1)} %all_to_all.11.in_ref, bf16[256,256]{1,0:T(8,128)(2,1)S(1)} %get-tuple-element.27.near_ref, f32[2,32,128]{2,1,0:T(8,128)S(1)} %get-tuple-element.28.far_ref), custom_call_target="tpu_custom_call" | custom-call | tf_op jit(solution)/shard_map/image/pallas_call | solution.py:481
Async XLA Ops:
  20.7 1.5 %collective-permute-start = (bf16[16,2,32,128]{3,2,1,0:T(8,128)(2,1)S(1)}, bf16[16,2,32,128]{3,2,1,0:T(8,128)(2,1)S(1)}, u32[]{:S(2)}, u32[]{:S(2)}) collective-permute-start(bf16[16,2,32,128]{3,2,1,0:T(8,128)(2,1)S(1)} %all_to_all.10.own_ref), channel_id=1, source_target_pairs={{0,1},{1,0},{2,3},{3,2},{4,5},{5,4},{6,7},{7,6},{8,9},{9,8},{10,11... | collective-permute-start | bytes 786440 | tf_op jit(solution)/shard_map/ppermute | solution.py:515
  24.4 1.6 %collective-permute-start.1 = (bf16[16,2,32,128]{3,2,1,0:T(8,128)(2,1)S(1)}, bf16[16,2,32,128]{3,2,1,0:T(8,128)(2,1)S(1)}, u32[]{:S(2)}, u32[]{:S(2)}) collective-permute-start(bf16[16,2,32,128]{3,2,1,0:T(8,128)(2,1)S(1)} %get-tuple-element.26), channel_id=1, source_target_pairs={{0,1},{1,0},{2,3},{3,2},{4,5},{5,4},{6,7},{7,6},{8,9},{9,8},{10,11... | collective-permute-start | bytes 786440 | tf_op jit(solution)/shard_map/ppermute | solution.py:515

commit v6 on v5

--- a/solution.py
+++ b/solution.py
@@ -88,69 +88,38 @@
     return (half * GROUP + inside % GROUP) * PATCH + inside // GROUP
 
 
-def column_kernel(
-    column_ref,
-    offsets_hbm,
-    image_hbm,
-    coords_hbm,
-    seen_hbm,
-    out_ref,
-    near_ref,
-    far_ref,
-    weights_ref,
-    coords_ref,
-    seen_ref,
-    left_ref,
-    offsets_ref,
-    small_sem,
-    image_sem,
-    later_sem,
-):
-    rows, extent = image_hbm.shape[2:]
-    far_count = extent // LANES
-    small = pltpu.make_async_copy(offsets_hbm, offsets_ref, small_sem)
-    small.start()
-    large = []
-    for ri in range(2):
-        copy = pltpu.make_async_copy(image_hbm.at[0, ri], left_ref.at[ri], image_sem.at[ri])
-        copy.start()
-        large.append(copy)
-    later = [
-        pltpu.make_async_copy(coords_hbm, coords_ref, later_sem.at[0]),
-        pltpu.make_async_copy(seen_hbm, seen_ref, later_sem.at[1]),
-    ]
-    for copy in later:
-        copy.start()
+def phase_kernel(column_ref, offsets_ref, near_ref, far_ref, weights_ref):
+    extent = far_ref.shape[1] * LANES
+    first = offsets_ref[pl.ds(lax.axis_index("facet"), 1), 1:2]
+    near, far = column_tables(column_ref[0], first, extent)
+    near_ref[...] = near_weights(near)
+    far_ref[0], far_ref[1] = far
     for h in range(SUBGRID // LANES):
         shape = (CONTRIB, LANES)
         tr, ti = cis(iota(shape, 0) * cell_of(iota(shape, 1) + h * LANES) * STEP)
         weights_ref[:, 2 * h * LANES : 2 * (h + 1) * LANES] = block([[tr, ti], [-ti, tr]]).astype(BF16)
-    small.wait()
-    first = offsets_ref[1, lax.axis_index("facet")]
-    near, far = column_tables(column_ref[0], first, extent)
-    near_ref[...] = near_weights(near)
-    far_ref[0], far_ref[1] = far
+
+
+def column_kernel(near_ref, far_ref, image_ref, out_ref):
+    rows, extent = image_ref.shape[2:]
+    far_count = extent // LANES
     real = jnp.zeros((rows, CONTRIB), F32)
     imag = jnp.zeros((rows, CONTRIB), F32)
-    for copy in large:
-        copy.wait()
     left = [
-        jnp.concatenate([left_ref[ri, :, pl.ds(y1 * LANES, LANES)] for ri in range(2)], axis=1)
+        jnp.concatenate([image_ref[0, ri, :, pl.ds(y1 * LANES, LANES)] for ri in range(2)], axis=1)
         for y1 in range(far_count)
     ]
     value = dot(jnp.concatenate(left, axis=0), near_ref[...])
     for y1 in range(far_count):
         part = value[y1 * rows : (y1 + 1) * rows]
-        here = slice(y1, y1 + 1)
-        pr, pi = times(part[:, :CONTRIB], part[:, CONTRIB:], far[0][here], far[1][here])
+        here = pl.ds(y1, 1)
+        pr, pi = times(part[:, :CONTRIB], part[:, CONTRIB:], far_ref[0, here], far_ref[1, here])
         real += pr
         imag += pi
     scale = 1.0 / math.sqrt(extent)
     both = jnp.stack([(real * scale).astype(BF16), (imag * scale).astype(BF16)])
     for member in range(out_ref.shape[0]):
         out_ref[member] = both
-    for copy in later:
-        copy.wait()
 
 
 def row_of(position):
@@ -177,8 +146,8 @@
     firsts = jnp.zeros(by_place, jnp.int32)
     lane_firsts = jnp.zeros(by_row, jnp.int32)
     for f in range(facets):
-        firsts = jnp.where(iota(by_place, 0) == f, offsets_ref[0, f], firsts)
-        lane_firsts = jnp.where(iota(by_row, 1) == f, offsets_ref[0, f], lane_firsts)
+        firsts = jnp.where(iota(by_place, 0) == f, offsets_ref[f, 0], firsts)
+        lane_firsts = jnp.where(iota(by_row, 1) == f, offsets_ref[f, 0], lane_firsts)
     place = firsts + iota(by_place, 1)
     place_real, place_imag = cis(
         -start * (place & MASK) - (CONTRIB - 1) * half_step * (place & (facet_rows - 1))
@@ -189,7 +158,7 @@
     )
     tables = []
     for f in range(facets):
-        shift = (facet_rows - offsets_ref[0, f] % facet_rows) % facet_rows
+        shift = (facet_rows - offsets_ref[f, 0] % facet_rows) % facet_rows
         rolled = pltpu.roll(kernel, shift, 1)
         real, imag = times(
             row_real[:, f : f + 1], row_imag[:, f : f + 1], place_real[f : f + 1], place_imag[f : f + 1]
@@ -207,8 +176,8 @@
 
 def table_kernel(
     piece_rows,
-    starts_hbm,
-    offsets_hbm,
+    starts_vmem,
+    offsets_vmem,
     coords_ref,
     rows_ref,
     shift_ref,
@@ -221,12 +190,12 @@
     sem,
 ):
     small = [
-        pltpu.make_async_copy(starts_hbm, starts_ref, sem.at[0]),
-        pltpu.make_async_copy(offsets_hbm, offsets_ref, sem.at[1]),
+        pltpu.make_async_copy(starts_vmem, starts_ref, sem.at[0]),
+        pltpu.make_async_copy(offsets_vmem, offsets_ref, sem.at[1]),
     ]
     for copy in small:
         copy.start()
-    facets = offsets_ref.shape[1]
+    facets = offsets_ref.shape[0]
     patch_rows = coords_ref.shape[1]
     block_rows = patch_rows * PATCH
     for p in range(patch_rows):
@@ -268,7 +237,7 @@
     shape = (facets, SUBGRID)
     firsts = jnp.zeros(shape, jnp.int32)
     for f in range(facets):
-        firsts = jnp.where(iota(shape, 0) == f, offsets_ref[1, f], firsts)
+        firsts = jnp.where(iota(shape, 0) == f, offsets_ref[f, 1], firsts)
     for ri, value in enumerate(cis(firsts * cell_of(iota(shape, 1)))):
         shift_ref[ri] = value * (1.0 / CONTRIB)
 
@@ -477,7 +446,7 @@
 VMEM = pl.BlockSpec(memory_space=pltpu.VMEM)
 
 
-def call(kernel, name, operands, in_specs, outs, scratch=(), out_specs=None):
+def call(kernel, name, operands, in_specs, outs, scratch=(), out_specs=None, flops=None):
     return pl.pallas_call(
         kernel,
         name=name,
@@ -485,6 +454,7 @@
         in_specs=in_specs,
         out_specs=out_specs or jax.tree.map(lambda _: VMEM, outs),
         scratch_shapes=list(scratch),
+        cost_estimate=flops and pl.CostEstimate(flops=flops, bytes_accessed=0, transcendentals=0),
         compiler_params=pltpu.CompilerParams(vmem_limit_bytes=40 * 1024 * 1024),
     )(*operands)
 
@@ -501,41 +471,35 @@
         [(2 * y + c) * facets + f for y in range(parts // 2) for f in range(facets)]
         for c in range(2)
     ]
-    offsets = facet_offsets.T
 
     def exchange(value):
         return lax.all_to_all(
             value, ("freq", "facet"), split_axis=0, concat_axis=0, axis_index_groups=groups, tiled=True
         )
 
-    def in_hbm(value):
-        return pltpu.with_memory_space_constraint(value, pltpu.HBM)
-
     def swap(value):
         return lax.ppermute(value, "freq", [(q, q ^ 1) for q in range(parts)])
 
     pieces = shape((members, 2, rows, CONTRIB), BF16)
     far_count = extent // LANES
-    transformed, near, far, weights, coords, seen = call(
-        column_kernel,
-        "column",
-        (column_offset, *map(in_hbm, (offsets, facet_image, uv_coords, observed))),
-        [SMEM] + [HBM] * 4,
+    near, far, weights = call(
+        phase_kernel,
+        "phase",
+        (column_offset, facet_offsets),
+        [SMEM, VMEM],
         (
-            pieces,
             shape((2 * LANES, 2 * CONTRIB), BF16),
             shape((2, far_count, CONTRIB), F32),
             shape((2 * CONTRIB, 2 * SUBGRID), BF16),
-            shape(uv_coords.shape, jnp.int32),
-            shape(observed.shape, BF16),
-        ),
-        (
-            pltpu.VMEM(facet_image.shape[1:], BF16),
-            pltpu.SMEM(offsets.shape, jnp.int32),
-            pltpu.SemaphoreType.DMA,
-            pltpu.SemaphoreType.DMA((2,)),
-            pltpu.SemaphoreType.DMA((2,)),
-        ),
+        ),
+        flops=200_000_000,
+    )
+    transformed = call(
+        column_kernel,
+        "column",
+        (near, far, facet_image),
+        [VMEM] * 3,
+        pieces,
     )
     own = exchange(transformed)
     other = swap(own)
@@ -544,8 +508,8 @@
     row_products, *tables = call(
         functools.partial(table_kernel, rows),
         "tables",
-        (in_hbm(subgrid_rows), in_hbm(offsets), coords),
-        [HBM, HBM, VMEM],
+        (subgrid_rows, facet_offsets, uv_coords),
+        [VMEM, VMEM, VMEM],
         (
             shape((facets, 2 * block_rows, 2 * parts * rows), BF16),
             shape((2, facets, SUBGRID), F32),
@@ -555,7 +519,7 @@
         ),
         (
             pltpu.SMEM(subgrid_rows.shape, jnp.int32),
-            pltpu.SMEM(offsets.shape, jnp.int32),
+            pltpu.SMEM(facet_offsets.shape, jnp.int32),
             pltpu.VMEM((facets * 2 * block_rows, parts * rows), BF16),
             pltpu.SemaphoreType.DMA((2,)),
         ),
@@ -563,7 +527,7 @@
     narrowed, give, residual_vis = call(
         grid_kernel,
         "grid",
-        (own, other, row_products, weights, *tables, seen),
+        (own, other, row_products, weights, *tables, observed),
         [VMEM] * 9,
         (
             shape((facets * block_rows, 2 * CONTRIB), BF16),

time: 40.9 us -> 40.5 us (level)
  Pallas kernels: 6.23 us -> 5.48 us
    pallas_call x5 -> x6, Pallas kernels: 6.23 us -> 5.48 us  [call(): pl.pallas_call(kernel, name=name, out_shape=outs, in_specs=in_specs, out_...]
where the time goes in v6:
time: 40.5 us; the launch traced here: 40.3 us
  blocking collectives  31.6 us (78%)
  Pallas kernels  5.48 us (14%)
  between operations  1.44 us (4%)
  waiting for transfers between devices  1.18 us (3%)
    all_to_all x2, blocking collectives, exchange(): lax.all_to_all(value, ('freq', 'facet'), split_axis=0, concat_axis=0, axi...  31.6 us
    pallas_call x6, Pallas kernels, call(): pl.pallas_call(kernel, name=name, out_shape=outs, in_specs=in_specs, out_...  5.48 us
    ppermute x2, waiting for transfers between devices, swap(): return lax.ppermute(value, 'freq', [(q, q ^ 1) for q in range(parts)])  1.18 us
  transfers between devices with their start and end apart: 2, of which 2 were waited for; matrix products, arithmetic and copies ran while one was open for 0% of the time, Pallas kernels for 4%

profile of v6, /device:TPU:0, one launch (start us, length us, event | category | flops | bytes accessed | tf_op | source)
XLA Modules:
  0.0 40.3 jit_solution(8399848761185014384)
XLA Ops:
  0.6 0.0 copy-start.4
  0.6 0.0 copy-start
  1.4 0.0 copy-done.4
  1.4 0.1 copy.8.offsets_vmem.offsets_ref
  1.4 0.4 phase.1
  1.8 0.0 copy-done
  1.8 0.4 column.1
  2.2 0.0 copy-start.1
  2.2 0.0 copy-start.3
  2.2 18.1 %all_to_all.10.own_ref = bf16[16,2,32,128]{3,2,1,0:T(8,128)(2,1)S(1)} all-to-all(bf16[16,2,32,128]{3,2,1,0:T(8,128)(2,1)S(1)} %column.1), channel_id=1, replica_groups={{0,4,8,12,16,20,24,28,2,6,10,14,18,22,26,30},{1,5,9,13,17,21,25,29,3,7,..., dimensions={0} | all-to-all | bytes 524288 | tf_op jit(solution)/shard_map/all_to_all | solution.py:476
  20.3 0.0 copy-start.2
  20.3 0.0 collective-permute-start
  20.3 0.0 copy-done.1
  20.3 0.0 copy-done.3
  20.4 1.3 %tables.1 = (bf16[8,128,256]{2,1,0:T(8,128)(2,1)S(1)}, f32[2,8,256]{2,1,0:T(8,128)S(1)}, f32[2,2,2,64,512]{4,3,2,1,0:T(8,128)S(1)}, f32[2,2,2,8,512]{4,3,2,1,0:T(8,128)S(1)}, bf16[2,2,256,512]{3,2,1,0:T(8,128)(2,1)S(1)}) custom-call(s32[8]{0:T(128)S(1)} %copy-done.3, s32[8,2]{1,0:T(8,128)S(1)} %copy.8.offsets_vmem.offsets_ref, s32[2,2,8,512]{3,2,1,0:T(8,128)S(1)} %copy-done.1), custom_call_target="tpu_custom_call" | custom-call | tf_op jit(solution)/shard_map/tables/pallas_call | solution.py:450
  21.7 0.2 collective-permute-done.other_ref
  21.9 0.0 copy-done.2
  21.9 2.1 %grid.1 = (bf16[512,256]{1,0:T(8,128)(2,1)S(1)}, bf16[16,2,32,128]{3,2,1,0:T(8,128)(2,1)S(1)}, bf16[2,2,8,512]{3,2,1,0:T(8,128)(2,1)}) custom-call(bf16[16,2,32,128]{3,2,1,0:T(8,128)(2,1)S(1)} %all_to_all.10.own_ref, bf16[16,2,32,128]{3,2,1,0:T(8,128)(2,1)S(1)} %collective-permute-done.other_ref, bf16[8,128,256]{2,1,0:T(8,128)(2,1)S(1)} %get-tuple-element.13.rows_ref, ...), custom_call_target="tpu_custom_call" | custom-call | tf_op jit(solution)/shard_map/grid/pallas_call | solution.py:450
  24.0 0.4 collective-permute-start.1
  24.3 0.3 keep.1
  24.6 1.0 %collective-permute-done.1 = bf16[16,2,32,128]{3,2,1,0:T(8,128)(2,1)S(1)} collective-permute-done((bf16[16,2,32,128]{3,2,1,0:T(8,128)(2,1)S(1)}, bf16[16,2,32,128]{3,2,1,0:T(8,128)(2,1)S(1)}, u32[]{:S(2)}, u32[]{:S(2)}) %collective-permute-start.1) | collective-permute-done | bytes 262176 | tf_op jit(solution)/shard_map/ppermute | solution.py:481
  25.6 0.1 add_convert_fusion
  25.7 13.5 %all_to_all.11.in_ref = bf16[16,2,32,128]{3,2,1,0:T(8,128)(2,1)S(1)} all-to-all(bf16[16,2,32,128]{3,2,1,0:T(8,128)(2,1)S(1)} %add_convert_fusion), channel_id=1, replica_groups={{0,4,8,12,16,20,24,28,2,6,10,14,18,22,26,30},{1,5,9,13,17,21,25,29,3,7,..., dimensions={0} | all-to-all | bytes 524288 | tf_op jit(solution)/shard_map/all_to_all | solution.py:476
  39.2 1.1 %image.1 = bf16[1,2,32,4096]{3,2,1,0:T(8,128)(2,1)} custom-call(bf16[16,2,32,128]{3,2,1,0:T(8,128)(2,1)S(1)} %all_to_all.11.in_ref, bf16[256,256]{1,0:T(8,128)(2,1)S(1)} %get-tuple-element.14.near_ref, f32[2,32,128]{2,1,0:T(8,128)S(1)} %get-tuple-element.15.far_ref), custom_call_target="tpu_custom_call" | custom-call | tf_op jit(solution)/shard_map/image/pallas_call | solution.py:450
Async XLA Ops:
  0.6 0.7 %copy-start.4 = (s32[8,2]{0,1:T(2,128)S(1)}, s32[8,2]{0,1:T(2,128)}, u32[]{:S(2)}) copy-start(s32[8,2]{0,1:T(2,128)} %param.7) | copy-start | bytes 196
  0.6 1.2 %copy-start = (bf16[1,2,32,4096]{3,2,1,0:T(8,128)(2,1)S(1)}, bf16[1,2,32,4096]{3,2,1,0:T(8,128)(2,1)}, u32[]{:S(2)}) copy-start(bf16[1,2,32,4096]{3,2,1,0:T(8,128)(2,1)} %image_ref.1) | copy-start | bytes 1572868
  2.2 18.2 %copy-start.1 = (s32[2,2,8,512]{3,2,1,0:T(8,128)S(1)}, s32[2,2,8,512]{3,2,1,0:T(8,128)}, u32[]{:S(2)}) copy-start(s32[2,2,8,512]{3,2,1,0:T(8,128)} %coords_ref.1) | copy-start | bytes 196612
  2.2 18.2 %copy-start.3 = (s32[8]{0:T(128)S(1)}, s32[8]{0:T(128)}, u32[]{:S(2)}) copy-start(s32[8]{0:T(128)} %starts_vmem.1) | copy-start | bytes 100
  20.3 1.5 %copy-start.2 = (bf16[2,2,8,512]{3,2,1,0:T(8,128)(2,1)S(1)}, bf16[2,2,8,512]{3,2,1,0:T(8,128)(2,1)}, u32[]{:S(2)}) copy-start(bf16[2,2,8,512]{3,2,1,0:T(8,128)(2,1)} %seen_ref.1) | copy-start | bytes 98308
  20.3 1.5 %collective-permute-start = (bf16[16,2,32,128]{3,2,1,0:T(8,128)(2,1)S(1)}, bf16[16,2,32,128]{3,2,1,0:T(8,128)(2,1)S(1)}, u32[]{:S(2)}, u32[]{:S(2)}) collective-permute-start(bf16[16,2,32,128]{3,2,1,0:T(8,128)(2,1)S(1)} %all_to_all.10.own_ref), channel_id=1, source_target_pairs={{0,1},{1,0},{2,3},{3,2},{4,5},{5,4},{6,7},{7,6},{8,9},{9,8},{10,11... | collective-permute-start | bytes 786440 | tf_op jit(solution)/shard_map/ppermute | solution.py:481
  24.0 1.6 %collective-permute-start.1 = (bf16[16,2,32,128]{3,2,1,0:T(8,128)(2,1)S(1)}, bf16[16,2,32,128]{3,2,1,0:T(8,128)(2,1)S(1)}, u32[]{:S(2)}, u32[]{:S(2)}) collective-permute-start(bf16[16,2,32,128]{3,2,1,0:T(8,128)(2,1)S(1)} %get-tuple-element.22), channel_id=1, source_target_pairs={{0,1},{1,0},{2,3},{3,2},{4,5},{5,4},{6,7},{7,6},{8,9},{9,8},{10,11... | collective-permute-start | bytes 786440 | tf_op jit(solution)/shard_map/ppermute | solution.py:481

commit v7 on v6

--- a/solution.py
+++ b/solution.py
@@ -220,17 +220,26 @@
         copy.wait()
     facet_rows = rows_ref.shape[2] // 2
     tables = row_tables(starts_ref, offsets_ref, facets, block_rows, facet_rows)
-    for f, (mr, mi) in enumerate(tables):
-        plain_ref[f * 2 * block_rows : (2 * f + 1) * block_rows] = mr.astype(BF16)
-        plain_ref[(2 * f + 1) * block_rows : (f + 1) * 2 * block_rows] = mi.astype(BF16)
+    kinds = [range(kind, facets, 2) for kind in range(2)]
+    height = 2 * block_rows
+    for at, f in enumerate([f for kind in kinds for f in kind]):
+        mr, mi = tables[f]
+        plain_ref[at * height : at * height + block_rows] = mr.astype(BF16)
+        plain_ref[at * height + block_rows : (at + 1) * height] = mi.astype(BF16)
     shape = (facet_rows, facet_rows)
     half, inside = iota(shape, 1) // (facet_rows // 2), iota(shape, 1) % (facet_rows // 2)
-    core = (lax.axis_index("freq") + half) % 2
-    place = (2 * (inside // piece_rows) + core) * piece_rows + inside % piece_rows
-    order = (iota(shape, 0) == place).astype(F32).astype(BF16)
-    ordered = dot(plain_ref[...], order).astype(BF16)
+    ordered = {}
+    top = 0
+    for kind, members in enumerate(kinds):
+        core = (lax.axis_index("freq") + lax.axis_index("facet") + kind + half) % 2
+        place = (2 * (inside // piece_rows) + core) * piece_rows + inside % piece_rows
+        order = (iota(shape, 0) == place).astype(F32).astype(BF16)
+        made = dot(plain_ref[top : top + len(members) * height], order).astype(BF16)
+        top += len(members) * height
+        for at, f in enumerate(members):
+            ordered[f] = made[at * height : (at + 1) * height]
     for f in range(facets):
-        here = ordered[f * 2 * block_rows : (f + 1) * 2 * block_rows]
+        here = ordered[f]
         rows_ref[f, :, :facet_rows] = here
         rows_ref[f, :block_rows, facet_rows:] = -here[block_rows:]
         rows_ref[f, block_rows:, facet_rows:] = here[:block_rows]
@@ -468,7 +477,7 @@
     block_rows = uv_coords.shape[1] * PATCH
     members = facets * parts // 2
     groups = [
-        [(2 * y + c) * facets + f for y in range(parts // 2) for f in range(facets)]
+        [(2 * y + (c + f) % 2) * facets + f for y in range(parts // 2) for f in range(facets)]
         for c in range(2)
     ]
 

time: 40.5 us -> 40.3 us (level)
  transfers between devices with their start and end apart: 2 -> 2, of which waited for: 2 -> 1; matrix products, arithmetic and copies ran while one was open for 0% -> 0% of each run, Pallas kernels for 4% -> 4%
where the time goes in v7:
time: 40.3 us; the launch traced here: 40.1 us
  blocking collectives  31.4 us (78%)
  Pallas kernels  5.5 us (14%)
  between operations  1.44 us (4%)
  waiting for transfers between devices  0.97 us (2%)
  starting transfers between devices  0.57 us (1%)
    all_to_all x2, blocking collectives, exchange(): lax.all_to_all(value, ('freq', 'facet'), split_axis=0, concat_axis=0, axi...  31.4 us
    pallas_call x6, Pallas kernels, call(): pl.pallas_call(kernel, name=name, out_shape=outs, in_specs=in_specs, out_...  5.5 us
    ppermute x2, waiting for transfers between devices, swap(): return lax.ppermute(value, 'freq', [(q, q ^ 1) for q in range(parts)])  0.97 us
  transfers between devices with their start and end apart: 2, of which 1 were waited for; matrix products, arithmetic and copies ran while one was open for 0% of the time, Pallas kernels for 4%

profile of v7, /device:TPU:0, one launch (start us, length us, event | category | flops | bytes accessed | tf_op | source)
XLA Modules:
  0.0 40.1 jit_solution(13695770375475311236)
XLA Ops:
  0.6 0.0 copy-start.4
  0.6 0.0 copy-start
  1.4 0.0 copy-done.4
  1.4 0.1 copy.8.offsets_vmem.offsets_ref
  1.4 0.4 phase.1
  1.8 0.0 copy-done
  1.8 0.4 column.1
  2.2 0.0 copy-start.1
  2.2 0.0 copy-start.3
  2.2 18.0 %all_to_all.10.own_ref = bf16[16,2,32,128]{3,2,1,0:T(8,128)(2,1)S(1)} all-to-all(bf16[16,2,32,128]{3,2,1,0:T(8,128)(2,1)S(1)} %column.1), channel_id=1, replica_groups={{0,5,8,13,16,21,24,29,2,7,10,15,18,23,26,31},{1,4,9,12,17,20,25,28,3,6,..., dimensions={0} | all-to-all | bytes 524288 | tf_op jit(solution)/shard_map/all_to_all | solution.py:485
  20.2 0.0 copy-start.2
  20.2 0.2 collective-permute-start
  20.4 0.0 copy-done.1
  20.4 0.0 copy-done.3
  20.4 1.3 %tables.1 = (bf16[8,128,256]{2,1,0:T(8,128)(2,1)S(1)}, f32[2,8,256]{2,1,0:T(8,128)S(1)}, f32[2,2,2,64,512]{4,3,2,1,0:T(8,128)S(1)}, f32[2,2,2,8,512]{4,3,2,1,0:T(8,128)S(1)}, bf16[2,2,256,512]{3,2,1,0:T(8,128)(2,1)S(1)}) custom-call(s32[8]{0:T(128)S(1)} %copy-done.3, s32[8,2]{1,0:T(8,128)S(1)} %copy.8.offsets_vmem.offsets_ref, s32[2,2,8,512]{3,2,1,0:T(8,128)S(1)} %copy-done.1), custom_call_target="tpu_custom_call" | custom-call | tf_op jit(solution)/shard_map/tables/pallas_call | solution.py:459
  21.8 0.0 collective-permute-done.other_ref
  21.8 0.0 copy-done.2
  21.8 2.1 %grid.1 = (bf16[512,256]{1,0:T(8,128)(2,1)S(1)}, bf16[16,2,32,128]{3,2,1,0:T(8,128)(2,1)S(1)}, bf16[2,2,8,512]{3,2,1,0:T(8,128)(2,1)}) custom-call(bf16[16,2,32,128]{3,2,1,0:T(8,128)(2,1)S(1)} %all_to_all.10.own_ref, bf16[16,2,32,128]{3,2,1,0:T(8,128)(2,1)S(1)} %collective-permute-done.other_ref, bf16[8,128,256]{2,1,0:T(8,128)(2,1)S(1)} %get-tuple-element.13.rows_ref, ...), custom_call_target="tpu_custom_call" | custom-call | tf_op jit(solution)/shard_map/grid/pallas_call | solution.py:459
  23.9 0.4 collective-permute-start.1
  24.3 0.3 keep.1
  24.5 1.0 %collective-permute-done.1 = bf16[16,2,32,128]{3,2,1,0:T(8,128)(2,1)S(1)} collective-permute-done((bf16[16,2,32,128]{3,2,1,0:T(8,128)(2,1)S(1)}, bf16[16,2,32,128]{3,2,1,0:T(8,128)(2,1)S(1)}, u32[]{:S(2)}, u32[]{:S(2)}) %collective-permute-start.1) | collective-permute-done | bytes 262176 | tf_op jit(solution)/shard_map/ppermute | solution.py:490
  25.5 0.1 add_convert_fusion
  25.6 13.4 %all_to_all.11.in_ref = bf16[16,2,32,128]{3,2,1,0:T(8,128)(2,1)S(1)} all-to-all(bf16[16,2,32,128]{3,2,1,0:T(8,128)(2,1)S(1)} %add_convert_fusion), channel_id=1, replica_groups={{0,5,8,13,16,21,24,29,2,7,10,15,18,23,26,31},{1,4,9,12,17,20,25,28,3,6,..., dimensions={0} | all-to-all | bytes 524288 | tf_op jit(solution)/shard_map/all_to_all | solution.py:485
  39.0 1.1 %image.1 = bf16[1,2,32,4096]{3,2,1,0:T(8,128)(2,1)} custom-call(bf16[16,2,32,128]{3,2,1,0:T(8,128)(2,1)S(1)} %all_to_all.11.in_ref, bf16[256,256]{1,0:T(8,128)(2,1)S(1)} %get-tuple-element.14.near_ref, f32[2,32,128]{2,1,0:T(8,128)S(1)} %get-tuple-element.15.far_ref), custom_call_target="tpu_custom_call" | custom-call | tf_op jit(solution)/shard_map/image/pallas_call | solution.py:459
Async XLA Ops:
  0.6 0.7 %copy-start.4 = (s32[8,2]{0,1:T(2,128)S(1)}, s32[8,2]{0,1:T(2,128)}, u32[]{:S(2)}) copy-start(s32[8,2]{0,1:T(2,128)} %param.7) | copy-start | bytes 196
  0.6 1.2 %copy-start = (bf16[1,2,32,4096]{3,2,1,0:T(8,128)(2,1)S(1)}, bf16[1,2,32,4096]{3,2,1,0:T(8,128)(2,1)}, u32[]{:S(2)}) copy-start(bf16[1,2,32,4096]{3,2,1,0:T(8,128)(2,1)} %image_ref.1) | copy-start | bytes 1572868
  2.2 18.3 %copy-start.1 = (s32[2,2,8,512]{3,2,1,0:T(8,128)S(1)}, s32[2,2,8,512]{3,2,1,0:T(8,128)}, u32[]{:S(2)}) copy-start(s32[2,2,8,512]{3,2,1,0:T(8,128)} %coords_ref.1) | copy-start | bytes 196612
  2.2 18.3 %copy-start.3 = (s32[8]{0:T(128)S(1)}, s32[8]{0:T(128)}, u32[]{:S(2)}) copy-start(s32[8]{0:T(128)} %starts_vmem.1) | copy-start | bytes 100
  20.2 1.5 %copy-start.2 = (bf16[2,2,8,512]{3,2,1,0:T(8,128)(2,1)S(1)}, bf16[2,2,8,512]{3,2,1,0:T(8,128)(2,1)}, u32[]{:S(2)}) copy-start(bf16[2,2,8,512]{3,2,1,0:T(8,128)(2,1)} %seen_ref.1) | copy-start | bytes 98308
  20.2 1.5 %collective-permute-start = (bf16[16,2,32,128]{3,2,1,0:T(8,128)(2,1)S(1)}, bf16[16,2,32,128]{3,2,1,0:T(8,128)(2,1)S(1)}, u32[]{:S(2)}, u32[]{:S(2)}) collective-permute-start(bf16[16,2,32,128]{3,2,1,0:T(8,128)(2,1)S(1)} %all_to_all.10.own_ref), channel_id=1, source_target_pairs={{0,1},{1,0},{2,3},{3,2},{4,5},{5,4},{6,7},{7,6},{8,9},{9,8},{10,11... | collective-permute-start | bytes 786440 | tf_op jit(solution)/shard_map/ppermute | solution.py:490
  23.9 1.6 %collective-permute-start.1 = (bf16[16,2,32,128]{3,2,1,0:T(8,128)(2,1)S(1)}, bf16[16,2,32,128]{3,2,1,0:T(8,128)(2,1)S(1)}, u32[]{:S(2)}, u32[]{:S(2)}) collective-permute-start(bf16[16,2,32,128]{3,2,1,0:T(8,128)(2,1)S(1)} %get-tuple-element.22), channel_id=1, source_target_pairs={{0,1},{1,0},{2,3},{3,2},{4,5},{5,4},{6,7},{7,6},{8,9},{9,8},{10,11... | collective-permute-start | bytes 786440 | tf_op jit(solution)/shard_map/ppermute | solution.py:490

commit v8 on v7

--- a/solution.py
+++ b/solution.py
@@ -231,7 +231,8 @@
     ordered = {}
     top = 0
     for kind, members in enumerate(kinds):
-        core = (lax.axis_index("freq") + lax.axis_index("facet") + kind + half) % 2
+        pair = lax.axis_index("freq") // 2 + inside // piece_rows
+        core = (lax.axis_index("freq") + lax.axis_index("facet") + kind + half + pair) % 2
         place = (2 * (inside // piece_rows) + core) * piece_rows + inside % piece_rows
         order = (iota(shape, 0) == place).astype(F32).astype(BF16)
         made = dot(plain_ref[top : top + len(members) * height], order).astype(BF16)
@@ -477,7 +478,7 @@
     block_rows = uv_coords.shape[1] * PATCH
     members = facets * parts // 2
     groups = [
-        [(2 * y + (c + f) % 2) * facets + f for y in range(parts // 2) for f in range(facets)]
+        [(2 * y + (c + f + y) % 2) * facets + f for y in range(parts // 2) for f in range(facets)]
         for c in range(2)
     ]
 

time: 40.3 us -> 41 us (1.017)
  blocking collectives: 31.4 us -> 32.1 us
    all_to_all x2, blocking collectives: 31.4 us -> 32.1 us  [exchange(): lax.all_to_all(value, ('freq', 'facet'), split_axis=0, concat_axis=0, axi...]
  transfers between devices with their start and end apart: 2 -> 2, of which waited for: 1 -> 2; matrix products, arithmetic and copies ran while one was open for 0% -> 0% of each run, Pallas kernels for 4% -> 4%
where the time goes in v8:
time: 41 us; the launch traced here: 40.8 us
  blocking collectives  32.1 us (78%)
  Pallas kernels  5.5 us (13%)
  between operations  1.44 us (4%)
  waiting for transfers between devices  1.14 us (3%)
    all_to_all x2, blocking collectives, exchange(): lax.all_to_all(value, ('freq', 'facet'), split_axis=0, concat_axis=0, axi...  32.1 us
    pallas_call x6, Pallas kernels, call(): pl.pallas_call(kernel, name=name, out_shape=outs, in_specs=in_specs, out_...  5.5 us
    ppermute x2, waiting for transfers between devices, swap(): return lax.ppermute(value, 'freq', [(q, q ^ 1) for q in range(parts)])  1.14 us
  transfers between devices with their start and end apart: 2, of which 2 were waited for; matrix products, arithmetic and copies ran while one was open for 0% of the time, Pallas kernels for 4%

profile of v8, /device:TPU:0, one launch (start us, length us, event | category | flops | bytes accessed | tf_op | source)
XLA Modules:
  0.0 40.8 jit_solution(10243038278624795389)
XLA Ops:
  0.6 0.0 copy-start.4
  0.6 0.0 copy-start
  1.4 0.0 copy-done.4
  1.4 0.1 copy.8.offsets_vmem.offsets_ref
  1.4 0.4 phase.1
  1.8 0.0 copy-done
  1.8 0.4 column.1
  2.2 0.0 copy-start.1
  2.2 0.0 copy-start.3
  2.2 18.3 %all_to_all.10.own_ref = bf16[16,2,32,128]{3,2,1,0:T(8,128)(2,1)S(1)} all-to-all(bf16[16,2,32,128]{3,2,1,0:T(8,128)(2,1)S(1)} %column.1), channel_id=1, replica_groups={{0,5,8,13,16,21,24,29,3,6,11,14,19,22,27,30},{1,4,9,12,17,20,25,28,2,7,..., dimensions={0} | all-to-all | bytes 524288 | tf_op jit(solution)/shard_map/all_to_all | solution.py:486
  20.5 0.0 copy-start.2
  20.5 0.0 collective-permute-start
  20.5 0.0 copy-done.1
  20.5 0.0 copy-done.3
  20.6 1.3 %tables.1 = (bf16[8,128,256]{2,1,0:T(8,128)(2,1)S(1)}, f32[2,8,256]{2,1,0:T(8,128)S(1)}, f32[2,2,2,64,512]{4,3,2,1,0:T(8,128)S(1)}, f32[2,2,2,8,512]{4,3,2,1,0:T(8,128)S(1)}, bf16[2,2,256,512]{3,2,1,0:T(8,128)(2,1)S(1)}) custom-call(s32[8]{0:T(128)S(1)} %copy-done.3, s32[8,2]{1,0:T(8,128)S(1)} %copy.8.offsets_vmem.offsets_ref, s32[2,2,8,512]{3,2,1,0:T(8,128)S(1)} %copy-done.1), custom_call_target="tpu_custom_call" | custom-call | tf_op jit(solution)/shard_map/tables/pallas_call | solution.py:460
  21.9 0.2 collective-permute-done.other_ref
  22.1 0.0 copy-done.2
  22.1 2.1 %grid.1 = (bf16[512,256]{1,0:T(8,128)(2,1)S(1)}, bf16[16,2,32,128]{3,2,1,0:T(8,128)(2,1)S(1)}, bf16[2,2,8,512]{3,2,1,0:T(8,128)(2,1)}) custom-call(bf16[16,2,32,128]{3,2,1,0:T(8,128)(2,1)S(1)} %all_to_all.10.own_ref, bf16[16,2,32,128]{3,2,1,0:T(8,128)(2,1)S(1)} %collective-permute-done.other_ref, bf16[8,128,256]{2,1,0:T(8,128)(2,1)S(1)} %get-tuple-element.13.rows_ref, ...), custom_call_target="tpu_custom_call" | custom-call | tf_op jit(solution)/shard_map/grid/pallas_call | solution.py:460
  24.2 0.4 collective-permute-start.1
  24.6 0.3 keep.1
  24.8 0.9 %collective-permute-done.1 = bf16[16,2,32,128]{3,2,1,0:T(8,128)(2,1)S(1)} collective-permute-done((bf16[16,2,32,128]{3,2,1,0:T(8,128)(2,1)S(1)}, bf16[16,2,32,128]{3,2,1,0:T(8,128)(2,1)S(1)}, u32[]{:S(2)}, u32[]{:S(2)}) %collective-permute-start.1) | collective-permute-done | bytes 262176 | tf_op jit(solution)/shard_map/ppermute | solution.py:491
  25.8 0.1 add_convert_fusion
  25.9 13.8 %all_to_all.11.in_ref = bf16[16,2,32,128]{3,2,1,0:T(8,128)(2,1)S(1)} all-to-all(bf16[16,2,32,128]{3,2,1,0:T(8,128)(2,1)S(1)} %add_convert_fusion), channel_id=1, replica_groups={{0,5,8,13,16,21,24,29,3,6,11,14,19,22,27,30},{1,4,9,12,17,20,25,28,2,7,..., dimensions={0} | all-to-all | bytes 524288 | tf_op jit(solution)/shard_map/all_to_all | solution.py:486
  39.6 1.1 %image.1 = bf16[1,2,32,4096]{3,2,1,0:T(8,128)(2,1)} custom-call(bf16[16,2,32,128]{3,2,1,0:T(8,128)(2,1)S(1)} %all_to_all.11.in_ref, bf16[256,256]{1,0:T(8,128)(2,1)S(1)} %get-tuple-element.14.near_ref, f32[2,32,128]{2,1,0:T(8,128)S(1)} %get-tuple-element.15.far_ref), custom_call_target="tpu_custom_call" | custom-call | tf_op jit(solution)/shard_map/image/pallas_call | solution.py:460
Async XLA Ops:
  0.6 0.7 %copy-start.4 = (s32[8,2]{0,1:T(2,128)S(1)}, s32[8,2]{0,1:T(2,128)}, u32[]{:S(2)}) copy-start(s32[8,2]{0,1:T(2,128)} %param.7) | copy-start | bytes 196
  0.6 1.2 %copy-start = (bf16[1,2,32,4096]{3,2,1,0:T(8,128)(2,1)S(1)}, bf16[1,2,32,4096]{3,2,1,0:T(8,128)(2,1)}, u32[]{:S(2)}) copy-start(bf16[1,2,32,4096]{3,2,1,0:T(8,128)(2,1)} %image_ref.1) | copy-start | bytes 1572868
  2.2 18.4 %copy-start.1 = (s32[2,2,8,512]{3,2,1,0:T(8,128)S(1)}, s32[2,2,8,512]{3,2,1,0:T(8,128)}, u32[]{:S(2)}) copy-start(s32[2,2,8,512]{3,2,1,0:T(8,128)} %coords_ref.1) | copy-start | bytes 196612
  2.2 18.4 %copy-start.3 = (s32[8]{0:T(128)S(1)}, s32[8]{0:T(128)}, u32[]{:S(2)}) copy-start(s32[8]{0:T(128)} %starts_vmem.1) | copy-start | bytes 100
  20.5 1.5 %copy-start.2 = (bf16[2,2,8,512]{3,2,1,0:T(8,128)(2,1)S(1)}, bf16[2,2,8,512]{3,2,1,0:T(8,128)(2,1)}, u32[]{:S(2)}) copy-start(bf16[2,2,8,512]{3,2,1,0:T(8,128)(2,1)} %seen_ref.1) | copy-start | bytes 98308
  20.5 1.5 %collective-permute-start = (bf16[16,2,32,128]{3,2,1,0:T(8,128)(2,1)S(1)}, bf16[16,2,32,128]{3,2,1,0:T(8,128)(2,1)S(1)}, u32[]{:S(2)}, u32[]{:S(2)}) collective-permute-start(bf16[16,2,32,128]{3,2,1,0:T(8,128)(2,1)S(1)} %all_to_all.10.own_ref), channel_id=1, source_target_pairs={{0,1},{1,0},{2,3},{3,2},{4,5},{5,4},{6,7},{7,6},{8,9},{9,8},{10,11... | collective-permute-start | bytes 786440 | tf_op jit(solution)/shard_map/ppermute | solution.py:491
  24.2 1.6 %collective-permute-start.1 = (bf16[16,2,32,128]{3,2,1,0:T(8,128)(2,1)S(1)}, bf16[16,2,32,128]{3,2,1,0:T(8,128)(2,1)S(1)}, u32[]{:S(2)}, u32[]{:S(2)}) collective-permute-start(bf16[16,2,32,128]{3,2,1,0:T(8,128)(2,1)S(1)} %get-tuple-element.22), channel_id=1, source_target_pairs={{0,1},{1,0},{2,3},{3,2},{4,5},{5,4},{6,7},{7,6},{8,9},{9,8},{10,11... | collective-permute-start | bytes 786440 | tf_op jit(solution)/shard_map/ppermute | solution.py:491
